TPU v7x, 32 devices: a whole 2x2x4 slice. The times are simulated.
32 devices in a mesh: grp: 2 (over x), req: 4 (over z), chan: 4 (over y, core).
Axes of the slice: x: 2, y: 2, z: 4, core: 2. Of those that a mesh axis runs over, the one named last changes fastest.
Arguments:
- tokens: bfloat16 [64, 4096], P(('grp', 'req'), 'chan'), parts along dimension 0, may hold values from -48 to 48
- rec_gain: bfloat16 [4096], P('chan'), may hold values from 0.099609375 to 1.8984375
- rec_in_weight: bfloat16 [2, 4096, 4096], P(None, 'chan', 'req'), may hold values from -0.09375 to 0.09375
- conv_weight: bfloat16 [4, 4096], P(None, 'req'), may hold values from -3 to 3
- conv_bias: bfloat16 [4096], P('req'), may hold values from -3 to 3
- conv_state: bfloat16 [3, 64, 4096], P(None, ('grp', 'chan'), 'req'), parts along dimension 1, may hold values from -5 to 5
- gate_weight: bfloat16 [2, 16, 256, 256], P(None, 'req'), may hold values from -0.375 to 0.375
- gate_bias: bfloat16 [2, 4096], P(None, 'req'), may hold values from -4 to 4
- lru_param: float32 [4096], P('req'), may hold values from -6 to -2
- lru_state: float32 [64, 4096], P(('grp', 'chan'), 'req'), parts along dimension 0, may hold values from -5 to 5
- rec_out_weight: bfloat16 [4096, 4096], P('req', 'chan'), may hold values from -0.09375 to 0.09375
- attn_gain: bfloat16 [4096], P('chan'), may hold values from 0.099609375 to 1.8984375
- query_weight: bfloat16 [4096, 4096], P('chan', 'req'), may hold values from -0.09375 to 0.09375
- kv_weight: bfloat16 [4096, 512], P('chan'), may hold values from -0.09375 to 0.09375
- key_cache: bfloat16 [64, 2048, 256], P(('grp', 'req', 'chan')), parts along dimension 0, may hold values from -400 to 400, as said below
- value_cache: bfloat16 [64, 2048, 256], P(('grp', 'req', 'chan')), parts along dimension 0, may hold values from -5 to 5
- lengths: int32 [64], P(('grp', 'req', 'chan')), parts along dimension 0, may hold values from 1 to 2047, as said below
- write_slots: int32 [64], P(('grp', 'req', 'chan')), parts along dimension 0, may hold values from 0 to 2047, as said below
- attn_out_weight: bfloat16 [4096, 4096], P('req', 'chan'), may hold values from -0.09375 to 0.09375
- mlp_gain: bfloat16 [4096], P('chan'), may hold values from 0.099609375 to 1.8984375
- mlp_in_weight: bfloat16 [2, 4096, 12288], P(None, 'chan', 'req'), may hold values from -0.09375 to 0.09375
- mlp_out_weight: bfloat16 [12288, 4096], P('req', 'chan'), may hold values from -0.0546875 to 0.0546875
Outputs:
- out_tokens: bfloat16 [64, 4096], P(('grp', 'req'), 'chan'), parts along dimension 0
- new_state: float32 [64, 4096], P(('grp', 'chan'), 'req'), parts along dimension 0
- new_entries: bfloat16 [64, 512], P(('grp', 'req', 'chan')), parts along dimension 0
There are 2 independent parts, one for each index of `grp`. A program takes and returns all parts, laid end to end along the dimension named above; an argument that names none is the same for every part. Nothing has to cross between parts.
Inputs may be any that keep to these rules, and one draw needn't show every extreme that they name: `key_cache`: keys as stored, already rotated. `lengths`: earlier tokens of a request that its cache holds. `write_slots`: slot that the new token overwrites; the used slots are the lengths entries just before it, cyclically.
All inputs are finite; a program needn't handle non-finite values.
Results may differ from a plain program's by a relative error of at most 0.011.
Values may be sent and summed in bfloat16 or wider, within the bound.
No kernel may reach another device: no remote copies, remote signals or barrier semaphores. Data moves between devices by JAX's collectives and lax.ppermute only.
A program may use at most 128 MiB of HBM per device.

v0:
```python
import jax
import jax.numpy as jnp
from jax import lax
from jax.sharding import PartitionSpec as P

EPS = 1e-06


def norm_rows(stream, gain):
    features = stream.shape[1] * lax.axis_size("chan")
    partial_value = jnp.sum(stream * stream, axis=1)
    summed = lax.psum(partial_value, "chan")
    factor = lax.rsqrt(summed / features + EPS)
    return (stream * factor[:, None] * gain.astype(jnp.float32)).astype(jnp.bfloat16)


def return_rows(partial_value):
    return lax.psum_scatter(partial_value, "req", scatter_dimension=0, tiled=True)


def rotate(vector, position):
    half = vector.shape[-1] // 2
    freq = 10000.0 ** (-jnp.arange(half, dtype=jnp.float32) / half)
    angle = position[..., None] * freq
    cosine = jnp.cos(angle)
    sine = jnp.sin(angle)
    first = vector[..., :half]
    second = vector[..., half:]
    return jnp.concatenate(
        [first * cosine - second * sine, second * cosine + first * sine], axis=-1
    )


def per_device(
    tokens,
    rec_gain,
    rec_in_weight,
    conv_weight,
    conv_bias,
    conv_state,
    gate_weight,
    gate_bias,
    lru_param,
    lru_state,
    rec_out_weight,
    attn_gain,
    query_weight,
    kv_weight,
    key_cache,
    value_cache,
    lengths,
    write_slots,
    attn_out_weight,
    mlp_gain,
    mlp_in_weight,
    mlp_out_weight,
):
    req_count = lax.axis_size("req")
    chan_count = lax.axis_size("chan")
    stream = tokens.astype(jnp.float32)
    normed = norm_rows(stream, rec_gain)
    rec_partial = jnp.einsum(
        "rd,gdo->gro",
        lax.all_gather(normed, "req", axis=0, tiled=True),
        rec_in_weight,
        preferred_element_type=jnp.float32,
    )
    branches = lax.psum_scatter(rec_partial, "chan", scatter_dimension=1, tiled=True)
    branch_x = branches[0]
    branch_y = branches[1]
    taps = conv_weight.astype(jnp.float32)
    convolved = taps[0] * branch_x + conv_bias.astype(jnp.float32)
    for offset in range(conv_state.shape[0]):
        convolved = convolved + taps[offset + 1] * conv_state[offset].astype(jnp.float32)
    rows_here = convolved.shape[0]
    lru_here = convolved.shape[1]
    blocks_here = gate_weight.shape[1]
    conv_low = convolved.astype(jnp.bfloat16).reshape(rows_here, blocks_here, -1)
    gates = jnp.einsum("rhi,ghio->grho", conv_low, gate_weight, preferred_element_type=jnp.float32)
    gates = gates.reshape(2, rows_here, lru_here) + gate_bias.astype(jnp.float32)[:, None, :]
    log_decay = -8.0 * jax.nn.sigmoid(gates[0]) * jax.nn.softplus(lru_param)[None, :]
    new_state = jnp.exp(log_decay) * lru_state + jnp.sqrt(1.0 - jnp.exp(2.0 * log_decay)) * (
        jax.nn.sigmoid(gates[1]) * convolved
    )
    mixed = (new_state * jax.nn.gelu(branch_y, approximate=True)).astype(jnp.bfloat16)
    rec_return = jnp.dot(
        lax.all_gather(mixed, "chan", axis=0, tiled=True),
        rec_out_weight,
        preferred_element_type=jnp.float32,
    )
    stream = stream + return_rows(rec_return)
    normed = norm_rows(stream, attn_gain)
    local_rows = normed.shape[0]
    owner_rows = local_rows // chan_count
    kv_partial = jnp.dot(normed, kv_weight, preferred_element_type=jnp.float32).reshape(
        chan_count, owner_rows, -1
    )
    key_value = lax.psum_scatter(kv_partial, "chan", scatter_dimension=0, tiled=True)[0]
    query_partial = jnp.dot(
        lax.all_gather(normed, "req", axis=0, tiled=True),
        query_weight,
        preferred_element_type=jnp.float32,
    )
    heads_here = query_partial.shape[1]
    arrived = lax.all_to_all(
        query_partial.reshape(req_count * chan_count, 1, owner_rows, heads_here),
        ("req", "chan"),
        split_axis=0,
        concat_axis=1,
        tiled=True,
    )
    summed = jnp.sum(arrived.reshape(req_count, chan_count, owner_rows, heads_here), axis=1)
    query = (
        summed.astype(jnp.bfloat16).transpose(1, 0, 2).reshape(owner_rows, req_count * heads_here)
    )
    head_dim = key_value.shape[1] // 2
    position = lengths.astype(jnp.float32)
    query_rot = rotate(
        query.astype(jnp.float32).reshape(owner_rows, -1, head_dim), position[:, None]
    )
    query_rot = (query_rot * head_dim ** (-0.5)).astype(jnp.bfloat16)
    key_new = rotate(key_value[:, :head_dim], position).astype(jnp.bfloat16)
    value_new = key_value[:, head_dim:].astype(jnp.bfloat16)
    scores = jnp.einsum("rhd,rjd->rhj", query_rot, key_cache, preferred_element_type=jnp.float32)
    self_score = jnp.einsum("rhd,rd->rh", query_rot, key_new, preferred_element_type=jnp.float32)
    window = key_cache.shape[1]
    slot_age = (write_slots[:, None] - jnp.arange(window, dtype=jnp.int32)[None, :]) % window
    is_valid = (slot_age >= 1) & (slot_age <= lengths[:, None])
    masked = jnp.where(is_valid[:, None, :], scores, -1e30)
    row_top = jnp.maximum(jnp.max(masked, axis=2), self_score)
    weights = jnp.exp(masked - row_top[..., None])
    self_weight = jnp.exp(self_score - row_top)
    row_total = jnp.sum(weights, axis=2) + self_weight
    weights_low = (weights / row_total[..., None]).astype(jnp.bfloat16)
    self_low = (self_weight / row_total).astype(jnp.bfloat16)
    attended = jnp.einsum(
        "rhj,rjd->rhd", weights_low, value_cache, preferred_element_type=jnp.float32
    )
    attended = (
        attended
        + self_low.astype(jnp.float32)[..., None] * value_new.astype(jnp.float32)[:, None, :]
    )
    attended = attended.astype(jnp.bfloat16).reshape(1, owner_rows, req_count, heads_here)
    head_groups = lax.all_to_all(attended, "req", split_axis=2, concat_axis=0, tiled=True)
    head_groups = head_groups.reshape(req_count, 1, owner_rows, heads_here)
    attn_return = jnp.einsum(
        "acrk,kd->acrd",
        lax.all_gather(head_groups, "chan", axis=1, tiled=True),
        attn_out_weight,
        preferred_element_type=jnp.float32,
    )
    stream = stream + return_rows(attn_return.reshape(-1, attn_return.shape[-1]))
    normed = norm_rows(stream, mlp_gain)
    pair_partial = jnp.einsum(
        "rd,gdo->gro",
        lax.all_gather(normed, "req", axis=0, tiled=True),
        mlp_in_weight,
        preferred_element_type=jnp.float32,
    )
    shares = lax.psum_scatter(pair_partial, "chan", scatter_dimension=1, tiled=True)
    hidden = (jax.nn.gelu(shares[0], approximate=True) * shares[1]).astype(jnp.bfloat16)
    down_part = jnp.dot(
        lax.all_gather(hidden, "chan", axis=0, tiled=True),
        mlp_out_weight,
        preferred_element_type=jnp.float32,
    )
    stream = stream + return_rows(down_part)
    new_entries = jnp.concatenate([key_new, value_new], axis=1)
    return (stream.astype(jnp.bfloat16), new_state, new_entries)


def solution(mesh):
    return jax.shard_map(
        per_device,
        mesh=mesh,
        in_specs=(
            P(("grp", "req"), "chan"),
            P("chan"),
            P(None, "chan", "req"),
            P(None, "req"),
            P("req"),
            P(None, ("grp", "chan"), "req"),
            P(None, "req", None, None),
            P(None, "req"),
            P("req"),
            P(("grp", "chan"), "req"),
            P("req", "chan"),
            P("chan"),
            P("chan", "req"),
            P("chan", None),
            P(("grp", "req", "chan"), None, None),
            P(("grp", "req", "chan"), None, None),
            P(("grp", "req", "chan")),
            P(("grp", "req", "chan")),
            P("req", "chan"),
            P("chan"),
            P(None, "chan", "req"),
            P("req", "chan"),
        ),
        out_specs=(
            P(("grp", "req"), "chan"),
            P(("grp", "chan"), "req"),
            P(("grp", "req", "chan"), None),
        ),
        check_vma=False,
    )
```

profile of v0, /device:TPU:0, one launch (start us, length us, event | category | flops | bytes accessed | tf_op | source)
XLA Modules:
  0.0 254.8 jit_solution(1636843034418048203)
XLA Ops:
  8.2 8.4 %psum.21 = f32[8]{0:T(128)S(1)} all-reduce(f32[8]{0:T(128)S(1)} %fusion.19), channel_id=1, replica_groups=mesh['grp'=2,'req'=4,'chan'=4] {'chan'}, use_global_device_ids=true, to_apply=%region_1.0 | all-reduce | flops 8 | bytes 64 | tf_op jit(solution)/shard_map/psum | solution.py:12
  18.1 13.4 %all_gather.18 = bf16[32,1024]{1,0:T(8,128)(2,1)S(1)} all-gather(bf16[8,1024]{1,0:T(8,128)(2,1)S(1)} %fusion.21), channel_id=1, replica_groups=mesh['grp'=2,'req'=4,'chan'=4] {'req'}, dimensions={0}, use_global_device_ids=true | all-gather | bytes 81920 | tf_op jit(solution)/shard_map/all_gather | solution.py:64
  31.5 3.8 %convolution_bitcast_fusion.1 = f32[2,32,1024]{2,1,0:T(8,128)} fusion(bf16[2,1024,1024]{2,1,0:T(8,128)(2,1)} %param.24, bf16[32,1024]{1,0:T(8,128)(2,1)S(1)} %all_gather.18), kind=kOutput, calls=%fused_computation.4 | convolution fusion | flops 134217728 | bytes 4521984 | tf_op jit(solution)/shard_map/rd,gdo->gro/dot_general | solution.py:62
  35.7 19.9 %reduce-scatter.6.cloned.1.call-done = f32[2,8,1024]{2,1,0:T(8,128)} async-done(((f32[2,32,1024]{2,1,0:T(8,128)}), f32[2,8,1024]{2,1,0:T(8,128)}) %reduce-scatter.6.cloned.1.call-update) | async-done | bytes 65552 | tf_op jit(solution)/shard_map/reduce_scatter | solution.py:68
  58.3 5.2 %all_gather.19 = bf16[32,1024]{1,0:T(8,128)(2,1)S(1)} all-gather(bf16[8,1024]{1,0:T(8,128)(2,1)S(1)} %get-tuple-element.11), channel_id=1, replica_groups=mesh['grp'=2,'req'=4,'chan'=4] {'chan'}, dimensions={0}, use_global_device_ids=true | all-gather | bytes 81920 | tf_op jit(solution)/shard_map/all_gather | solution.py:87
  63.5 2.7 %fusion.73 = f32[32,1024]{1,0:T(8,128)} fusion(bf16[32,1024]{1,0:T(8,128)(2,1)S(1)} %all_gather.19, bf16[1024,1024]{1,0:T(8,128)(2,1)} %param.32), kind=kOutput, calls=%fused_computation.128 | convolution fusion | flops 67108864 | bytes 2293760 | tf_op jit(solution)/shard_map/dot_general | solution.py:86
  66.4 19.4 %reduce-scatter.8.cloned.1.call-done = f32[8,1024]{1,0:T(8,128)} async-done(((f32[32,1024]{1,0:T(8,128)}), f32[8,1024]{1,0:T(8,128)}) %reduce-scatter.8.cloned.1.call-update) | async-done | bytes 32784 | tf_op jit(solution)/shard_map/reduce_scatter | solution.py:18
  87.3 5.6 %psum.22 = f32[8]{0:T(128)S(1)} all-reduce(f32[8]{0:T(128)S(1)} %multiply_reduce_fusion.1), channel_id=1, replica_groups=mesh['grp'=2,'req'=4,'chan'=4] {'chan'}, use_global_device_ids=true, to_apply=%region_5.6 | all-reduce | flops 8 | bytes 64 | tf_op jit(solution)/shard_map/psum | solution.py:12
  93.7 13.2 %all_gather.20 = bf16[32,1024]{1,0:T(8,128)(2,1)S(1)} all-gather(bf16[8,1024]{1,0:T(8,128)(2,1)S(1)} %multiply_convert_fusion.1), channel_id=1, replica_groups=mesh['grp'=2,'req'=4,'chan'=4] {'req'}, dimensions={0}, use_global_device_ids=true | all-gather | bytes 81920 | tf_op jit(solution)/shard_map/all_gather | solution.py:100
  107.2 10.1 %all-reduce = f32[4,2,512]{2,1,0:T(2,128)S(1)} all-reduce(f32[4,2,512]{2,1,0:T(2,128)S(1)} %reshape.216), channel_id=5, replica_groups=mesh['grp'=2,'req'=4,'chan'=4] {'chan'}, use_global_device_ids=true, to_apply=%region_8.9.clone | all-reduce | flops 4096 | bytes 32768
  117.3 2.1 fusion.74
  120.1 3.5 %all-to-all-start = ((f32[16,1,2,1024]{3,2,1,0:T(2,128)}), f32[16,1,2,1024]{3,2,1,0:T(2,128)S(1)}, u32[]{:S(2)}, u32[]{:S(2)}) async-start(f32[16,1,2,1024]{3,2,1,0:T(2,128)} %bitcast.21), calls=%async_computation.2 | async-start | bytes 262144 | tf_op jit(solution)/shard_map/all_to_all | solution.py:105
  124.4 7.0 %all-to-all-done = f32[16,1,2,1024]{3,2,1,0:T(2,128)S(1)} async-done(((f32[16,1,2,1024]{3,2,1,0:T(2,128)}), f32[16,1,2,1024]{3,2,1,0:T(2,128)S(1)}, u32[]{:S(2)}, u32[]{:S(2)}) %all-to-all-start) | async-done | bytes 131104 | tf_op jit(solution)/shard_map/all_to_all | solution.py:105
  133.7 8.0 %all_to_all.24 = bf16[1,2,4,1024]{3,1,0,2:T(2,128)(2,1)S(1)} all-to-all(bf16[1,2,4,1024]{3,1,0,2:T(2,128)(2,1)S(1)} %copy.37), channel_id=1, replica_groups=mesh['grp'=2,'req'=4,'chan'=4] {'req'}, dimensions={2} | all-to-all | bytes 32768 | tf_op jit(solution)/shard_map/all_to_all | solution.py:144
  141.6 5.2 %all-gather = bf16[4,4,2,1,1024]{4,0,3,2,1:T(4,128)(2,1)S(1)} all-gather(bf16[4,1,2,1,1024]{4,0,3,2,1:T(4,128)(2,1)S(1)} %bitcast.127), channel_id=2, replica_groups=mesh['grp'=2,'req'=4,'chan'=4] {'chan'}, dimensions={1}, use_global_device_ids=true | all-gather | bytes 81920 | tf_op jit(solution)/shard_map/all_gather | solution.py:148
  146.9 2.1 fusion
  149.8 16.8 %reduce-scatter.10.cloned.1.call-done = f32[8,1024]{1,0:T(8,128)} async-done(((f32[32,1024]{1,0:T(8,128)}), f32[8,1024]{1,0:T(8,128)}) %reduce-scatter.10.cloned.1.call-update) | async-done | bytes 32784 | tf_op jit(solution)/shard_map/reduce_scatter | solution.py:18
  167.5 5.7 %psum.23 = f32[8]{0:T(128)S(1)} all-reduce(f32[8]{0:T(128)S(1)} %get-tuple-element.7), channel_id=1, replica_groups=mesh['grp'=2,'req'=4,'chan'=4] {'chan'}, use_global_device_ids=true, to_apply=%region_12.13 | all-reduce | flops 8 | bytes 64 | tf_op jit(solution)/shard_map/psum | solution.py:12
  173.3 13.2 %all_gather.22 = bf16[32,1024]{1,0:T(8,128)(2,1)S(1)} all-gather(bf16[8,1024]{1,0:T(8,128)(2,1)S(1)} %multiply_convert_fusion), channel_id=1, replica_groups=mesh['grp'=2,'req'=4,'chan'=4] {'req'}, dimensions={0}, use_global_device_ids=true | all-gather | bytes 81920 | tf_op jit(solution)/shard_map/all_gather | solution.py:156
  186.5 7.7 %convolution_bitcast_fusion = f32[2,32,3072]{2,1,0:T(8,128)} fusion(bf16[2,1024,3072]{2,1,0:T(8,128)(2,1)} %param.42, bf16[32,1024]{1,0:T(8,128)(2,1)S(1)} %all_gather.22), kind=kOutput, calls=%fused_computation | convolution fusion | flops 402653184 | bytes 13434880 | tf_op jit(solution)/shard_map/rd,gdo->gro/dot_general | solution.py:154
  194.3 21.8 %reduce-scatter.12.cloned.1.call-done = f32[2,8,3072]{2,1,0:T(8,128)} async-done(((f32[2,32,3072]{2,1,0:T(8,128)}), f32[2,8,3072]{2,1,0:T(8,128)}) %reduce-scatter.12.cloned.1.call-update) | async-done | bytes 196624 | tf_op jit(solution)/shard_map/reduce_scatter | solution.py:160
  217.0 5.6 %all_gather.23 = bf16[32,3072]{1,0:T(8,128)(2,1)S(1)} all-gather(bf16[8,3072]{1,0:T(8,128)(2,1)S(1)} %fusion.15), channel_id=1, replica_groups=mesh['grp'=2,'req'=4,'chan'=4] {'chan'}, dimensions={0}, use_global_device_ids=true | all-gather | bytes 245760 | tf_op jit(solution)/shard_map/all_gather | solution.py:163
  222.6 4.6 %fusion.76 = f32[32,1024]{1,0:T(8,128)} fusion(bf16[32,3072]{1,0:T(8,128)(2,1)S(1)} %all_gather.23, bf16[3072,1024]{1,0:T(8,128)(2,1)} %param.43), kind=kOutput, calls=%fused_computation.131 | convolution fusion | flops 201326592 | bytes 6619136 | tf_op jit(solution)/shard_map/dot_general | solution.py:162
  227.9 19.0 %reduce-scatter.14.cloned.1.call-done = f32[8,1024]{1,0:T(8,128)} async-done(((f32[32,1024]{1,0:T(8,128)}), f32[8,1024]{1,0:T(8,128)}) %reduce-scatter.14.cloned.1.call-update) | async-done | bytes 32784 | tf_op jit(solution)/shard_map/reduce_scatter | solution.py:18
  (102 shorter events, 16.5 us)
Async XLA Ops:
  7.2 124.6 %copy-start = (bf16[2,2048,256]{2,1,0:T(8,128)(2,1)S(1)}, bf16[2,2048,256]{2,1,0:T(8,128)(2,1)}, u32[]{:S(2)}) copy-start(bf16[2,2048,256]{2,1,0:T(8,128)(2,1)} %param.36) | copy-start | bytes 6291460
  7.2 48.4 %reduce-scatter.6.cloned.1.call-start = ((), (), s32[]{:S(2)}) async-start(), calls=%async_computation.7 | async-start | bytes 327680 | tf_op jit(solution)/shard_map/reduce_scatter | solution.py:68
  31.5 3.9 %copy-start.9 = (bf16[1024]{0:T(1024)(128)(2,1)S(1)}, bf16[1024]{0:T(1024)(128)(2,1)}, u32[]{:S(2)}) copy-start(bf16[1024]{0:T(1024)(128)(2,1)} %param.26) | copy-start | bytes 6148
  31.5 3.9 %copy-start.11 = (f32[1024]{0:T(1024)S(1)}, f32[1024]{0:T(1024)}, u32[]{:S(2)}) copy-start(f32[1024]{0:T(1024)} %param.30) | copy-start | bytes 12292
  31.5 4.0 %copy-start.10 = (bf16[2,1024]{1,0:T(2,128)(2,1)S(1)}, bf16[2,1024]{1,0:T(2,128)(2,1)}, u32[]{:S(2)}) copy-start(bf16[2,1024]{1,0:T(2,128)(2,1)} %param.29) | copy-start | bytes 12292
  31.5 4.0 %copy-start.7 = (bf16[4,1024]{1,0:T(4,128)(2,1)S(1)}, bf16[4,1024]{1,0:T(4,128)(2,1)}, u32[]{:S(2)}) copy-start(bf16[4,1024]{1,0:T(4,128)(2,1)} %param.25) | copy-start | bytes 24580
  31.5 4.1 %copy-start.6 = (bf16[3,8,1024]{2,1,0:T(8,128)(2,1)S(1)}, bf16[3,8,1024]{2,1,0:T(8,128)(2,1)}, u32[]{:S(2)}) copy-start(bf16[3,8,1024]{2,1,0:T(8,128)(2,1)} %param.27) | copy-start | bytes 147460
  31.5 24.9 %copy-start.2 = (bf16[2,4,256,256]{3,2,1,0:T(8,128)(2,1)S(1)}, bf16[2,4,256,256]{3,2,1,0:T(8,128)(2,1)}, u32[]{:S(2)}) copy-start(bf16[2,4,256,256]{3,2,1,0:T(8,128)(2,1)} %param.28) | copy-start | bytes 3145732
  35.3 21.4 %copy-start.8 = (f32[8,1024]{1,0:T(8,128)S(1)}, f32[8,1024]{1,0:T(8,128)}, u32[]{:S(2)}) copy-start(f32[8,1024]{1,0:T(8,128)} %param.31) | copy-start | bytes 98308
  35.4 50.4 %reduce-scatter.8.cloned.1.call-start = ((), (), s32[]{:S(2)}) async-start(), calls=%async_computation.8 | async-start | bytes 163840 | tf_op jit(solution)/shard_map/reduce_scatter | solution.py:18
  56.4 9.8 %copy-start.14 = (s32[2]{0:T(128)S(1)}, s32[2]{0:T(128)}, u32[]{:S(2)}) copy-start(s32[2]{0:T(128)} %param.39) | copy-start | bytes 28
  56.4 9.8 %copy-start.15 = (s32[2]{0:T(128)S(1)}, s32[2]{0:T(128)}, u32[]{:S(2)}) copy-start(s32[2]{0:T(128)} %param.38) | copy-start | bytes 28
  56.4 10.0 %copy-start.12 = (bf16[1024]{0:T(1024)(128)(2,1)S(1)}, bf16[1024]{0:T(1024)(128)(2,1)}, u32[]{:S(2)}) copy-start(bf16[1024]{0:T(1024)(128)(2,1)} %param.33) | copy-start | bytes 6148
  56.4 29.4 %copy-start.4 = (bf16[8,1024]{1,0:T(8,128)(2,1)S(1)}, bf16[8,1024]{1,0:T(8,128)(2,1)}, u32[]{:S(2)}) copy-start(bf16[8,1024]{1,0:T(8,128)(2,1)} %param.22) | copy-start | bytes 49156
  56.4 30.3 %copy-start.16 = (u32[32]{0:T(128)S(1)}, u32[32]{0:T(128)}, u32[]{:S(2)}) copy-start(u32[32]{0:T(128)} %constant.61) | copy-start | bytes 388
  56.7 50.3 %copy-start.3 = (bf16[1024,512]{1,0:T(8,128)(2,1)S(1)}, bf16[1024,512]{1,0:T(8,128)(2,1)}, u32[]{:S(2)}) copy-start(bf16[1024,512]{1,0:T(8,128)(2,1)} %param.35) | copy-start | bytes 3145732
  120.1 11.4 %all-to-all-start = ((f32[16,1,2,1024]{3,2,1,0:T(2,128)}), f32[16,1,2,1024]{3,2,1,0:T(2,128)S(1)}, u32[]{:S(2)}, u32[]{:S(2)}) async-start(f32[16,1,2,1024]{3,2,1,0:T(2,128)} %bitcast.21), calls=%async_computation.2 | async-start | bytes 262144 | tf_op jit(solution)/shard_map/all_to_all | solution.py:105
  123.6 43.1 %reduce-scatter.10.cloned.1.call-start = ((), (), s32[]{:S(2)}) async-start(), calls=%async_computation.9 | async-start | bytes 163840 | tf_op jit(solution)/shard_map/reduce_scatter | solution.py:18
  131.6 1.6 copy-start.1
  146.9 2.9 %copy-start.13 = (bf16[1024]{0:T(1024)(128)(2,1)S(1)}, bf16[1024]{0:T(1024)(128)(2,1)}, u32[]{:S(2)}) copy-start(bf16[1024]{0:T(1024)(128)(2,1)} %param.41) | copy-start | bytes 6148
  146.9 19.8 %copy-start.5 = (f32[8,1024]{1,0:T(8,128)S(1)}, f32[8,1024]{1,0:T(8,128)}, u32[]{:S(2)}) copy-start(f32[8,1024]{1,0:T(8,128)} %reduce-scatter.8.cloned.1.call-done) | copy-start | bytes 98308
  149.8 66.3 %reduce-scatter.12.cloned.1.call-start = ((), (), s32[]{:S(2)}) async-start(), calls=%async_computation.10 | async-start | bytes 983040 | tf_op jit(solution)/shard_map/reduce_scatter | solution.py:160
  194.2 52.7 %reduce-scatter.14.cloned.1.call-start = ((), (), s32[]{:S(2)}) async-start(), calls=%async_computation.11 | async-start | bytes 163840 | tf_op jit(solution)/shard_map/reduce_scatter | solution.py:18
Sparse Core Ops, SparseCore 0:
  35.5 20.0 reduce-scatter.5
  66.3 19.4 reduce-scatter.7
  149.9 16.7 reduce-scatter.9
  194.3 21.6 reduce-scatter.11
  227.4 19.4 reduce-scatter.13
where the time goes:
time: 256 us; the launch traced here: 255 us
  waiting for transfers between devices  104 us (41%)
  blocking collectives  93.6 us (37%)
  matrix products  24.8 us (10%)
  between operations  14.2 us (6%)
  other arithmetic  10.2 us (4%)
  local copies, waits for them, and re-layouts  4.22 us (2%)
  starting transfers between devices  3.72 us (1%)
    reduce_scatter x3, waiting for transfers between devices, return_rows(): lax.psum_scatter(partial_value, 'req', scatter_dimension=0, tiled=True)  55.2 us
    all_gather x3, blocking collectives, per_device(): lax.all_gather(normed, 'req', axis=0, tiled=True)  39.8 us
    reduce_scatter x1, waiting for transfers between devices, per_device(): lax.psum_scatter(pair_partial, 'chan', scatter_dimension=1, tiled=True)  21.8 us
    reduce_scatter x1, waiting for transfers between devices, per_device(): lax.psum_scatter(rec_partial, 'chan', scatter_dimension=1, tiled=True)  19.9 us
    psum x3, blocking collectives, norm_rows(): summed = lax.psum(partial_value, 'chan')  19.7 us
    dot_general x2, matrix products, per_device(): jnp.einsum('rd,gdo->gro', lax.all_gather(normed, 'req', axis=0, tiled=Tru...  11.5 us
    unnamed x1, blocking collectives  10.1 us
    all_to_all x1, blocking collectives, per_device(): lax.all_to_all(attended, 'req', split_axis=2, concat_axis=0, tiled=True)  7.96 us
  transfers between devices with their start and end apart: 6, of which 6 were waited for; matrix products, arithmetic and copies ran while one was open for 1% of the time, Pallas kernels for 0%

commit v1 on v0

v1 whole, which is shorter than its diff:
```python
import jax
import jax.numpy as jnp
from jax import lax
from jax.sharding import PartitionSpec as P

EPS = 1e-06
F32 = jnp.float32
BF16 = jnp.bfloat16
LANES = 128


def swap(value, axis, mask):
    return lax.ppermute(value, axis, [(i, i ^ mask) for i in range(lax.axis_size(axis))])


def in_order(blocks, index):
    bit = 1
    while bit < len(blocks):
        flip = (index & bit) != 0
        blocks = [jnp.where(flip, blocks[b ^ bit], blocks[b]) for b in range(len(blocks))]
        bit *= 2
    return blocks


def gather_rows(value, axis):
    blocks = [value] + [swap(value, axis, m) for m in range(1, lax.axis_size(axis))]
    return jnp.concatenate(in_order(blocks, lax.axis_index(axis)), axis=0)


def exchange_sum(part, axis, masks):
    low = part.astype(BF16)
    total = part
    for m in masks:
        total = total + swap(low, axis, m).astype(F32)
    return total


def square_lanes(squares):
    high = lax.reduce_precision(squares, 8, 7)
    low = squares - high
    half = (squares.shape[0], LANES // 2)
    return jnp.concatenate(
        [jnp.broadcast_to(high[:, None], half), jnp.broadcast_to(low[:, None], half)], axis=1
    )


def factor_of(lanes, features):
    squares = lanes[..., 0] + lanes[..., LANES // 2]
    return lax.rsqrt(squares / features + EPS)


def scaled(stream, gain):
    return (stream * gain.astype(F32)).astype(BF16), jnp.sum(stream * stream, axis=1)


def rotate(vector, position):
    half = vector.shape[-1] // 2
    freq = 10000.0 ** (-jnp.arange(half, dtype=F32) / half)
    angle = position[..., None] * freq
    cosine = jnp.cos(angle)
    sine = jnp.sin(angle)
    first = vector[..., :half]
    second = vector[..., half:]
    return jnp.concatenate(
        [first * cosine - second * sine, second * cosine + first * sine], axis=-1
    )


def dot(a, b):
    return jnp.dot(a, b, preferred_element_type=F32)


def per_device(
    tokens,
    rec_gain,
    rec_in_weight,
    conv_weight,
    conv_bias,
    conv_state,
    gate_weight,
    gate_bias,
    lru_param,
    lru_state,
    rec_out_weight,
    attn_gain,
    query_weight,
    kv_weight,
    key_cache,
    value_cache,
    lengths,
    write_slots,
    attn_out_weight,
    mlp_gain,
    mlp_in_weight,
    mlp_out_weight,
):
    nr = lax.axis_size("req")
    nc = lax.axis_size("chan")
    row = lax.axis_index("req")
    col = lax.axis_index("chan")
    features = tokens.shape[1] * nc
    req_masks = range(1, nr)
    chan_masks = range(1, nc)
    tokens_all = gather_rows(tokens, "req").astype(F32)
    rows_all = tokens_all.shape[0]
    normed, squares = scaled(tokens_all, rec_gain)
    part = jnp.concatenate(
        [dot(normed, rec_in_weight[0]), dot(normed, rec_in_weight[1]), square_lanes(squares)],
        axis=1,
    ).reshape(nc, rows_all // nc, -1)
    total = lax.dynamic_index_in_dim(part, col, 0, keepdims=False)
    low = part.astype(BF16)
    for m in chan_masks:
        total = total + swap(
            lax.dynamic_index_in_dim(low, col ^ m, 0, keepdims=False), "chan", m
        ).astype(F32)
    lru_here = lru_state.shape[1]
    factor = factor_of(total[:, 2 * lru_here :], features)[:, None]
    branch_x = total[:, :lru_here] * factor
    branch_y = total[:, lru_here : 2 * lru_here] * factor
    taps = conv_weight.astype(F32)
    convolved = taps[0] * branch_x + conv_bias.astype(F32)
    for offset in range(conv_state.shape[0]):
        convolved = convolved + taps[offset + 1] * conv_state[offset].astype(F32)
    rows_here = convolved.shape[0]
    blocks_here = gate_weight.shape[1]
    conv_low = convolved.astype(BF16).reshape(rows_here, blocks_here, -1)
    gates = jnp.einsum("rhi,ghio->grho", conv_low, gate_weight, preferred_element_type=F32)
    gates = gates.reshape(2, rows_here, lru_here) + gate_bias.astype(F32)[:, None, :]
    log_decay = -8.0 * jax.nn.sigmoid(gates[0]) * jax.nn.softplus(lru_param)[None, :]
    new_state = jnp.exp(log_decay) * lru_state + jnp.sqrt(1.0 - jnp.exp(2.0 * log_decay)) * (
        jax.nn.sigmoid(gates[1]) * convolved
    )
    mixed = (new_state * jax.nn.gelu(branch_y, approximate=True)).astype(BF16)
    rec_return = dot(gather_rows(mixed, "chan"), rec_out_weight)
    stream = tokens_all + exchange_sum(rec_return, "req", req_masks)
    normed, squares = scaled(stream, attn_gain)
    kv_here = kv_weight.shape[1] // nr
    kv_slice = lax.dynamic_slice_in_dim(kv_weight, row * kv_here, kv_here, 1)
    owner_rows = rows_all // (nr * nc)
    heads_here = query_weight.shape[1]
    sent = jnp.concatenate(
        [dot(normed, query_weight), dot(normed, kv_slice), square_lanes(squares)], axis=1
    ).astype(BF16)
    arrived = lax.all_to_all(
        sent.reshape(nr * nc, owner_rows, -1),
        ("req", "chan"),
        split_axis=0,
        concat_axis=0,
        tiled=True,
    )
    summed = jnp.sum(arrived.astype(F32).reshape(nr, nc, owner_rows, -1), axis=1)
    factor = factor_of(summed[0, :, heads_here + kv_here :], features)[None, :, None]
    query = (summed[:, :, :heads_here] * factor).astype(BF16)
    query = query.transpose(1, 0, 2).reshape(owner_rows, nr * heads_here)
    key_value = (summed[:, :, heads_here : heads_here + kv_here] * factor).transpose(1, 0, 2)
    key_value = key_value.reshape(owner_rows, nr * kv_here)
    head_dim = key_value.shape[1] // 2
    position = lengths.astype(F32)
    query_rot = rotate(query.astype(F32).reshape(owner_rows, -1, head_dim), position[:, None])
    query_rot = (query_rot * head_dim ** (-0.5)).astype(BF16)
    key_new = rotate(key_value[:, :head_dim], position).astype(BF16)
    value_new = key_value[:, head_dim:].astype(BF16)
    scores = jnp.einsum("rhd,rjd->rhj", query_rot, key_cache, preferred_element_type=F32)
    self_score = jnp.einsum("rhd,rd->rh", query_rot, key_new, preferred_element_type=F32)
    window = key_cache.shape[1]
    slot_age = (write_slots[:, None] - jnp.arange(window, dtype=jnp.int32)[None, :]) % window
    is_valid = (slot_age >= 1) & (slot_age <= lengths[:, None])
    masked = jnp.where(is_valid[:, None, :], scores, -1e30)
    row_top = jnp.maximum(jnp.max(masked, axis=2), self_score)
    weights = jnp.exp(masked - row_top[..., None])
    self_weight = jnp.exp(self_score - row_top)
    row_total = jnp.sum(weights, axis=2) + self_weight
    weights_low = (weights / row_total[..., None]).astype(BF16)
    self_low = (self_weight / row_total).astype(BF16)
    attended = jnp.einsum("rhj,rjd->rhd", weights_low, value_cache, preferred_element_type=F32)
    attended = attended + self_low.astype(F32)[..., None] * value_new.astype(F32)[:, None, :]
    attended = attended.astype(BF16).reshape(owner_rows, nr, heads_here).transpose(1, 0, 2)
    attended = jnp.broadcast_to(attended[:, None], (nr, nc, owner_rows, heads_here))
    attended = lax.all_to_all(
        attended.reshape(nr * nc, owner_rows, heads_here),
        ("req", "chan"),
        split_axis=0,
        concat_axis=0,
        tiled=True,
    ).reshape(rows_all, heads_here)
    stream = stream + exchange_sum(dot(attended, attn_out_weight), "req", req_masks)
    normed, squares = scaled(stream, mlp_gain)
    cores = 2 if nc % 2 == 0 else 1
    hidden_here = mlp_in_weight.shape[2] // cores
    core = col % cores
    gate_part = dot(normed, mlp_in_weight[0]).reshape(rows_all, cores, hidden_here)
    up_part = dot(normed, mlp_in_weight[1]).reshape(rows_all, cores, hidden_here)
    lanes = square_lanes(squares)

    def half(index):
        return jnp.concatenate(
            [
                lax.dynamic_index_in_dim(gate_part, index, 1, keepdims=False),
                lax.dynamic_index_in_dim(up_part, index, 1, keepdims=False),
                lanes,
            ],
            axis=1,
        )

    total = half(core)
    if cores == 2:
        total = total + swap(half(core ^ 1).astype(BF16), "chan", 1).astype(F32)
    lanes = square_lanes(total[:, 2 * hidden_here] + total[:, 2 * hidden_here + LANES // 2])
    total = jnp.concatenate([total[:, : 2 * hidden_here], lanes], axis=1)
    total = exchange_sum(total, "chan", range(cores, nc, cores))
    factor = factor_of(total[:, 2 * hidden_here :], features)[:, None]
    hidden = jax.nn.gelu(total[:, :hidden_here] * factor, approximate=True) * (
        total[:, hidden_here : 2 * hidden_here] * factor
    )
    hidden = hidden.astype(BF16)
    if cores == 2:
        hidden = jnp.concatenate(in_order([hidden, swap(hidden, "chan", 1)], core), axis=1)
    down = dot(hidden, mlp_out_weight).reshape(nr, rows_all // nr, -1)
    down_low = down.astype(BF16)
    result = lax.dynamic_index_in_dim(stream.reshape(down.shape), row, 0, keepdims=False)
    result = result + lax.dynamic_index_in_dim(down, row, 0, keepdims=False)
    for m in req_masks:
        result = result + swap(
            lax.dynamic_index_in_dim(down_low, row ^ m, 0, keepdims=False), "req", m
        ).astype(F32)
    new_entries = jnp.concatenate([key_new, value_new], axis=1)
    return (result.astype(BF16), new_state, new_entries)


def solution(mesh):
    return jax.shard_map(
        per_device,
        mesh=mesh,
        in_specs=(
            P(("grp", "req"), "chan"),
            P("chan"),
            P(None, "chan", "req"),
            P(None, "req"),
            P("req"),
            P(None, ("grp", "chan"), "req"),
            P(None, "req", None, None),
            P(None, "req"),
            P("req"),
            P(("grp", "chan"), "req"),
            P("req", "chan"),
            P("chan"),
            P("chan", "req"),
            P("chan", None),
            P(("grp", "req", "chan"), None, None),
            P(("grp", "req", "chan"), None, None),
            P(("grp", "req", "chan")),
            P(("grp", "req", "chan")),
            P("req", "chan"),
            P("chan"),
            P(None, "chan", "req"),
            P("req", "chan"),
        ),
        out_specs=(
            P(("grp", "req"), "chan"),
            P(("grp", "chan"), "req"),
            P(("grp", "req", "chan"), None),
        ),
        check_vma=False,
    )
```

time: 256 us -> 133 us (0.52)
  blocking collectives: 93.6 us -> 9.48 us
  waiting for transfers between devices: 104 us -> 28.4 us
  local copies, waits for them, and re-layouts: 4.22 us -> 33.3 us
  starting transfers between devices: 3.72 us -> 26.8 us
  between operations: 14.2 us -> 1.05 us
    reduce_scatter x5 -> x0, waiting for transfers between devices: 96.9 us -> none  [the longest x3 55.2 us: return_rows(): lax.psum_scatter(partial_value, 'req', scatter_dimension=0, tiled=True)]
    all_gather x6 -> x0, blocking collectives: 55.8 us -> none  [the longest x3 39.8 us: per_device(): lax.all_gather(normed, 'req', axis=0, tiled=True)]
    dot_general x0 -> x3, local copies, waits for them, and re-layouts: none -> 27.6 us  [dot(): return jnp.dot(a, b, preferred_element_type=F32)]
    ppermute x0 -> x21, starting transfers between devices: none -> 23.2 us  [swap(): lax.ppermute(value, axis, [(i, i ^ mask) for i in range(lax.axis_size(axi...]
    ppermute x0 -> x21, waiting for transfers between devices: none -> 21.4 us  [swap(): lax.ppermute(value, axis, [(i, i ^ mask) for i in range(lax.axis_size(axi...]
    psum x3 -> x0, blocking collectives: 19.7 us -> none  [norm_rows(): summed = lax.psum(partial_value, 'chan')]
    unnamed x1 -> x0, blocking collectives: 10.1 us -> none
    convert_element_type x17 -> x15, other arithmetic: 6.35 us -> 4.58 us  [the longest x1 1.43 us: per_device(): mixed = (new_state * jax.nn.gelu(branch_y, approximate=True)).astype(BF16)]
  transfers between devices with their start and end apart: 6 -> 22, of which waited for: 6 -> 13; matrix products, arithmetic and copies ran while one was open for 1% -> 24% of each run, Pallas kernels for 0% -> 0%
where the time goes in v1:
time: 133 us; the launch traced here: 131 us
  local copies, waits for them, and re-layouts  33.3 us (25%)
  waiting for transfers between devices  28.4 us (21%)
  starting transfers between devices  26.8 us (20%)
  matrix products  23.7 us (18%)
  blocking collectives  9.48 us (7%)
  other arithmetic  8.81 us (7%)
    dot_general x3, local copies, waits for them, and re-layouts, dot(): return jnp.dot(a, b, preferred_element_type=F32)  27.6 us
    ppermute x21, starting transfers between devices, swap(): lax.ppermute(value, axis, [(i, i ^ mask) for i in range(lax.axis_size(axi...  23.2 us
    dot_general x9, matrix products, dot(): return jnp.dot(a, b, preferred_element_type=F32)  22.1 us
    ppermute x21, waiting for transfers between devices, swap(): lax.ppermute(value, axis, [(i, i ^ mask) for i in range(lax.axis_size(axi...  21.4 us
    all_to_all x1, blocking collectives, per_device(): lax.all_to_all(attended.reshape(nr * nc, owner_rows, heads_here), ('req',...  9.48 us
    all_to_all x1, waiting for transfers between devices, per_device(): lax.all_to_all(sent.reshape(nr * nc, owner_rows, -1), ('req', 'chan'), sp...  6.95 us
    all_to_all x1, starting transfers between devices, per_device(): lax.all_to_all(sent.reshape(nr * nc, owner_rows, -1), ('req', 'chan'), sp...  3.59 us
  transfers between devices with their start and end apart: 22, of which 13 were waited for; matrix products, arithmetic and copies ran while one was open for 24% of the time, Pallas kernels for 0%

profile of v1, /device:TPU:0, one launch (start us, length us, event | category | flops | bytes accessed | tf_op | source)
XLA Modules:
  0.0 131.5 jit_solution(2994375912623626369)
XLA Ops:
  0.6 5.1 %collective-permute-start = (bf16[8,1024]{1,0:T(8,128)(2,1)}, bf16[8,1024]{1,0:T(8,128)(2,1)S(1)}, u32[]{:S(2)}, u32[]{:S(2)}) collective-permute-start(bf16[8,1024]{1,0:T(8,128)(2,1)} %param.22), channel_id=1, source_target_pairs={{0,12},{4,8},{8,4},{12,0},{1,13},{5,9},{9,5},{13,1},{2,14},{6,10},... | collective-permute-start | bytes 49160 | tf_op jit(solution)/shard_map/ppermute | solution.py:13
  8.6 2.1 %collective-permute-done.1 = bf16[8,1024]{1,0:T(8,128)(2,1)S(1)} collective-permute-done((bf16[8,1024]{1,0:T(8,128)(2,1)}, bf16[8,1024]{1,0:T(8,128)(2,1)S(1)}, u32[]{:S(2)}, u32[]{:S(2)}) %collective-permute-start.1) | collective-permute-done | bytes 16416 | tf_op jit(solution)/shard_map/ppermute | solution.py:13
  11.4 2.7 %fusion.2 = f32[32,1024]{1,0:T(8,128)} fusion(bf16[2,1024,1024]{2,1,0:T(8,128)(2,1)} %param.24, f32[1024]{0:T(1024)S(1)} %convert_element_type.159, bf16[8,1024]{1,0:T(8,128)(2,1)S(1)} %get-tuple-element.32, bf16[8,1024]{1,0:T(8,128)(2,1)S(1)} %get-tuple-element.31, bf16[8,1024]{1,0:T(8,128)(2,1)S(1)} %get-tuple-element.30, ...), kind=kOutput, calls=%fused_computation.5 | convolution fusion | flops 67436544 | bytes 2297856 | tf_op jit(solution)/shard_map/dot_general | solution.py:70
  14.1 2.8 %fusion = f32[32,1024]{1,0:T(8,128)} fusion(bf16[2,1024,1024]{2,1,0:T(8,128)(2,1)} %param.24, f32[1024]{0:T(1024)S(1)} %convert_element_type.159, bf16[8,1024]{1,0:T(8,128)(2,1)S(1)} %get-tuple-element.32, bf16[8,1024]{1,0:T(8,128)(2,1)S(1)} %get-tuple-element.31, bf16[8,1024]{1,0:T(8,128)(2,1)S(1)} %get-tuple-element.30, ...), kind=kOutput, calls=%fused_computation.3 | convolution fusion | flops 67436544 | bytes 2297856 | tf_op jit(solution)/shard_map/dot_general | solution.py:70
  18.9 1.5 %collective-permute-start.4 = (bf16[8,2176]{1,0:T(8,128)(2,1)}, bf16[8,2176]{1,0:T(8,128)(2,1)}, u32[]{:S(2)}, u32[]{:S(2)}) collective-permute-start(bf16[8,2176]{1,0:T(8,128)(2,1)} %get-tuple-element.21), channel_id=1, source_target_pairs={{0,2},{1,3},{2,0},{3,1},{4,6},{5,7},{6,4},{7,5},{8,10},{9,11},{10,... | collective-permute-start | bytes 104456 | tf_op jit(solution)/shard_map/ppermute | solution.py:13
  30.0 1.6 %collective-permute-done.7 = bf16[8,1024]{1,0:T(8,128)(2,1)S(1)} collective-permute-done((bf16[8,1024]{1,0:T(8,128)(2,1)S(1)}, bf16[8,1024]{1,0:T(8,128)(2,1)S(1)}, u32[]{:S(2)}, u32[]{:S(2)}) %collective-permute-start.7) | collective-permute-done | bytes 16416 | tf_op jit(solution)/shard_map/ppermute | solution.py:13
  31.6 2.1 %fusion.108 = (bf16[32,1024]{1,0:T(8,128)(2,1)S(1)}, f32[32,1024]{1,0:T(8,128)S(1)}) fusion(bf16[1024,1024]{1,0:T(8,128)(2,1)} %param.32, bf16[8,1024]{1,0:T(8,128)(2,1)S(1)} %get-tuple-element.28, bf16[8,1024]{1,0:T(8,128)(2,1)S(1)} %get-tuple-element.27, bf16[8,1024]{1,0:T(8,128)(2,1)S(1)} %get-tuple-element.26, bf16[8,1024]{1,0:T(8,128)(2,1)S(1)} %get-tuple-element.25), kind=kOutput, calls=%fused_computation.198 | convolution fusion | flops 67403776 | bytes 2359296 | tf_op jit(solution)/shard_map/dot_general | solution.py:70
  33.7 1.8 %collective-permute-start.11 = (bf16[32,1024]{1,0:T(8,128)(2,1)S(1)}, bf16[32,1024]{1,0:T(8,128)(2,1)S(1)}, u32[]{:S(2)}, u32[]{:S(2)}) collective-permute-start(bf16[32,1024]{1,0:T(8,128)(2,1)S(1)} %get-tuple-element.53), channel_id=1, source_target_pairs={{0,12},{4,8},{8,4},{12,0},{1,13},{5,9},{9,5},{13,1},{2,14},{6,10},... | collective-permute-start | bytes 196616 | tf_op jit(solution)/shard_map/ppermute | solution.py:13
  35.9 2.3 %collective-permute-start.9 = (bf16[32,1024]{1,0:T(8,128)(2,1)S(1)}, bf16[32,1024]{1,0:T(8,128)(2,1)S(1)}, u32[]{:S(2)}, u32[]{:S(2)}) collective-permute-start(bf16[32,1024]{1,0:T(8,128)(2,1)S(1)} %get-tuple-element.53), channel_id=1, source_target_pairs={{0,4},{4,0},{8,12},{12,8},{1,5},{5,1},{9,13},{13,9},{2,6},{6,2},{1... | collective-permute-start | bytes 196616 | tf_op jit(solution)/shard_map/ppermute | solution.py:13
  38.2 2.3 %collective-permute-done.11 = bf16[32,1024]{1,0:T(8,128)(2,1)S(1)} collective-permute-done((bf16[32,1024]{1,0:T(8,128)(2,1)S(1)}, bf16[32,1024]{1,0:T(8,128)(2,1)S(1)}, u32[]{:S(2)}, u32[]{:S(2)}) %collective-permute-start.11) | collective-permute-done | bytes 65568 | tf_op jit(solution)/shard_map/ppermute | solution.py:13
  40.4 1.8 %collective-permute-done.10 = bf16[32,1024]{1,0:T(8,128)(2,1)S(1)} collective-permute-done((bf16[32,1024]{1,0:T(8,128)(2,1)S(1)}, bf16[32,1024]{1,0:T(8,128)(2,1)S(1)}, u32[]{:S(2)}, u32[]{:S(2)}) %collective-permute-start.10) | collective-permute-done | bytes 65568 | tf_op jit(solution)/shard_map/ppermute | solution.py:13
  42.4 2.1 %convolution_convert_fusion = bf16[32,1024]{1,0:T(8,128)(2,1)S(1)} fusion(bf16[1024,1024]{1,0:T(8,128)(2,1)} %param.34, f32[32,1024]{1,0:T(8,128)S(1)} %get-tuple-element.10, f32[1024]{0:T(1024)S(1)} %convert_element_type.179), kind=kOutput, calls=%fused_computation.10 | convolution fusion | flops 67207168 | bytes 2297856 | tf_op jit(solution)/shard_map/dot_general | solution.py:70
  46.7 3.6 %all-to-all-start = ((bf16[16,2,1280]{2,1,0:T(2,128)(2,1)}), bf16[16,2,1280]{2,1,0:T(2,128)(2,1)S(1)}, u32[]{:S(2)}, u32[]{:S(2)}) async-start(bf16[16,2,1280]{2,1,0:T(2,128)(2,1)} %concatenate.50), calls=%async_computation | async-start | bytes 163840 | tf_op jit(solution)/shard_map/all_to_all | solution.py:145
  50.5 7.0 %all-to-all-done = bf16[16,2,1280]{2,1,0:T(2,128)(2,1)S(1)} async-done(((bf16[16,2,1280]{2,1,0:T(2,128)(2,1)}), bf16[16,2,1280]{2,1,0:T(2,128)(2,1)S(1)}, u32[]{:S(2)}, u32[]{:S(2)}) %all-to-all-start) | async-done | bytes 81952 | tf_op jit(solution)/shard_map/all_to_all | solution.py:145
  60.0 9.5 %all_to_all.10 = bf16[16,2,1024]{2,1,0:T(2,128)(2,1)S(1)} all-to-all(bf16[16,2,1024]{2,1,0:T(2,128)(2,1)S(1)} %bitcast.132), channel_id=1, replica_groups=mesh['grp'=2,'req'=4,'chan'=4] {'req','chan'}, dimensions={0} | all-to-all | bytes 131072 | tf_op jit(solution)/shard_map/all_to_all | solution.py:180
  71.6 2.8 %collective-permute-start.12 = (bf16[32,1024]{1,0:T(8,128)(2,1)S(1)}, bf16[32,1024]{1,0:T(8,128)(2,1)S(1)}, u32[]{:S(2)}, u32[]{:S(2)}) collective-permute-start(bf16[32,1024]{1,0:T(8,128)(2,1)S(1)} %get-tuple-element.57), channel_id=1, source_target_pairs={{0,4},{4,0},{8,12},{12,8},{1,5},{5,1},{9,13},{13,9},{2,6},{6,2},{1... | collective-permute-start | bytes 196616 | tf_op jit(solution)/shard_map/ppermute | solution.py:13
  74.4 10.5 %slice_bitcast_fusion = (bf16[3072,1024]{0,1:T(8,128)(2,1)}, bf16[3072,1024]{0,1:T(8,128)(2,1)}) fusion(bf16[2,1024,3072]{2,1,0:T(8,128)(2,1)} %param.42), kind=kLoop, calls=%fused_computation | loop fusion | bytes 25165824 | tf_op jit(solution)/shard_map/dot_general | solution.py:70
  84.9 8.6 %copy.56 = bf16[3072,1024]{1,0:T(8,128)(2,1)} copy(bf16[3072,1024]{0,1:T(8,128)(2,1)} %get-tuple-element.15) | data formatting | bytes 12582912 | tf_op jit(solution)/shard_map/dot_general | solution.py:70
  93.5 8.5 %copy.55 = bf16[3072,1024]{1,0:T(8,128)(2,1)} copy(bf16[3072,1024]{0,1:T(8,128)(2,1)} %get-tuple-element.16) | data formatting | bytes 12582912 | tf_op jit(solution)/shard_map/dot_general | solution.py:70
  102.2 4.9 %fusion.79 = f32[32,2,1536]{2,0,1:T(8,128)S(1)} fusion(bf16[2,1536,1024]{2,1,0:T(8,128)(2,1)} %bitcast.128, f32[32,1024]{1,0:T(8,128)S(1)} %get-tuple-element.6, f32[1024]{0:T(1024)S(1)} %convert_element_type.196), kind=kOutput, calls=%fused_computation.157 | convolution fusion | flops 201392128 | bytes 6819840 | tf_op jit(solution)/shard_map/dot_general | solution.py:70
  107.1 1.9 %fusion.81 = f32[32,2,1536]{2,0,1:T(8,128)S(1)} fusion(bf16[2,1536,1024]{2,1,0:T(8,128)(2,1)S(1)} %bitcast.129, f32[32,1024]{1,0:T(8,128)S(1)} %get-tuple-element.6, f32[1024]{0:T(1024)S(1)} %convert_element_type.196), kind=kOutput, calls=%fused_computation.158 | convolution fusion | flops 201392128 | bytes 6819840 | tf_op jit(solution)/shard_map/dot_general | solution.py:70
  111.6 7.0 %collective-permute-done.16 = bf16[32,3200]{1,0:T(8,128)(2,1)S(1)} collective-permute-done((bf16[32,3200]{1,0:T(8,128)(2,1)S(1)}, bf16[32,3200]{1,0:T(8,128)(2,1)S(1)}, u32[]{:S(2)}, u32[]{:S(2)}) %collective-permute-start.16) | collective-permute-done | bytes 204832 | tf_op jit(solution)/shard_map/ppermute | solution.py:13
  120.5 4.1 %fusion.111 = (bf16[4,8,1024]{2,1,0:T(8,128)(2,1)S(1)}, f32[4,8,1024]{2,1,0:T(8,128)S(1)}) fusion(bf16[3072,1024]{1,0:T(8,128)(2,1)} %param.43, bf16[32,1536]{1,0:T(8,128)(2,1)S(1)} %get-tuple-element.18, bf16[32,1536]{1,0:T(8,128)(2,1)S(1)} %get-tuple-element.17), kind=kOutput, calls=%fused_computation.201 | convolution fusion | flops 201752576 | bytes 6684672 | tf_op jit(solution)/shard_map/dot_general | solution.py:70
  126.2 2.9 %collective-permute-start.18 = (bf16[8,1024]{1,0:T(8,128)(2,1)S(1)}, bf16[8,1024]{1,0:T(8,128)(2,1)S(1)}, u32[]{:S(2)}, u32[]{:S(2)}) collective-permute-start(bf16[8,1024]{1,0:T(8,128)(2,1)S(1)} %get-tuple-element.22), channel_id=1, source_target_pairs={{0,4},{4,0},{8,12},{12,8},{1,5},{5,1},{9,13},{13,9},{2,6},{6,2},{1... | collective-permute-start | bytes 49160 | tf_op jit(solution)/shard_map/ppermute | solution.py:13
  (135 shorter events, 31.1 us)
Async XLA Ops:
  0.6 57.6 %copy-start = (bf16[2,2048,256]{2,1,0:T(8,128)(2,1)S(1)}, bf16[2,2048,256]{2,1,0:T(8,128)(2,1)}, u32[]{:S(2)}) copy-start(bf16[2,2048,256]{2,1,0:T(8,128)(2,1)} %param.36) | copy-start | bytes 6291460
  0.6 7.9 %collective-permute-start = (bf16[8,1024]{1,0:T(8,128)(2,1)}, bf16[8,1024]{1,0:T(8,128)(2,1)S(1)}, u32[]{:S(2)}, u32[]{:S(2)}) collective-permute-start(bf16[8,1024]{1,0:T(8,128)(2,1)} %param.22), channel_id=1, source_target_pairs={{0,12},{4,8},{8,4},{12,0},{1,13},{5,9},{9,5},{13,1},{2,14},{6,10},... | collective-permute-start | bytes 49160 | tf_op jit(solution)/shard_map/ppermute | solution.py:13
  5.8 4.8 %collective-permute-start.1 = (bf16[8,1024]{1,0:T(8,128)(2,1)}, bf16[8,1024]{1,0:T(8,128)(2,1)S(1)}, u32[]{:S(2)}, u32[]{:S(2)}) collective-permute-start(bf16[8,1024]{1,0:T(8,128)(2,1)} %param.22), channel_id=1, source_target_pairs={{0,8},{4,12},{8,0},{12,4},{1,9},{5,13},{9,1},{13,5},{2,10},{6,14},... | collective-permute-start | bytes 49160 | tf_op jit(solution)/shard_map/ppermute | solution.py:13
  5.8 4.8 %collective-permute-start.2 = (bf16[8,1024]{1,0:T(8,128)(2,1)}, bf16[8,1024]{1,0:T(8,128)(2,1)S(1)}, u32[]{:S(2)}, u32[]{:S(2)}) collective-permute-start(bf16[8,1024]{1,0:T(8,128)(2,1)} %param.22), channel_id=1, source_target_pairs={{0,4},{4,0},{8,12},{12,8},{1,5},{5,1},{9,13},{13,9},{2,6},{6,2},{1... | collective-permute-start | bytes 49160 | tf_op jit(solution)/shard_map/ppermute | solution.py:13
  18.9 4.0 %collective-permute-start.5 = (bf16[8,2176]{1,0:T(8,128)(2,1)}, bf16[8,2176]{1,0:T(8,128)(2,1)}, u32[]{:S(2)}, u32[]{:S(2)}) collective-permute-start(bf16[8,2176]{1,0:T(8,128)(2,1)} %get-tuple-element.20), channel_id=1, source_target_pairs={{0,3},{1,2},{2,1},{3,0},{4,7},{5,6},{6,5},{7,4},{8,11},{9,10},{10,... | collective-permute-start | bytes 104456 | tf_op jit(solution)/shard_map/ppermute | solution.py:13
  18.9 4.4 %collective-permute-start.4 = (bf16[8,2176]{1,0:T(8,128)(2,1)}, bf16[8,2176]{1,0:T(8,128)(2,1)}, u32[]{:S(2)}, u32[]{:S(2)}) collective-permute-start(bf16[8,2176]{1,0:T(8,128)(2,1)} %get-tuple-element.21), channel_id=1, source_target_pairs={{0,2},{1,3},{2,0},{3,1},{4,6},{5,7},{6,4},{7,5},{8,10},{9,11},{10,... | collective-permute-start | bytes 104456 | tf_op jit(solution)/shard_map/ppermute | solution.py:13
  20.4 2.9 %collective-permute-start.3 = (bf16[8,2176]{1,0:T(8,128)(2,1)S(1)}, bf16[8,2176]{1,0:T(8,128)(2,1)}, u32[]{:S(2)}, u32[]{:S(2)}) collective-permute-start(bf16[8,2176]{1,0:T(8,128)(2,1)S(1)} %get-tuple-element.19), channel_id=1, source_target_pairs={{0,1},{1,0},{2,3},{3,2},{4,5},{5,4},{6,7},{7,6},{8,9},{9,8},{10,11... | collective-permute-start | bytes 104456 | tf_op jit(solution)/shard_map/ppermute | solution.py:13
  26.9 3.2 %collective-permute-start.6 = (bf16[8,1024]{1,0:T(8,128)(2,1)S(1)}, bf16[8,1024]{1,0:T(8,128)(2,1)S(1)}, u32[]{:S(2)}, u32[]{:S(2)}) collective-permute-start(bf16[8,1024]{1,0:T(8,128)(2,1)S(1)} %get-tuple-element.11), channel_id=1, source_target_pairs={{0,3},{1,2},{2,1},{3,0},{4,7},{5,6},{6,5},{7,4},{8,11},{9,10},{10,... | collective-permute-start | bytes 49160 | tf_op jit(solution)/shard_map/ppermute | solution.py:13
  27.9 3.7 %collective-permute-start.7 = (bf16[8,1024]{1,0:T(8,128)(2,1)S(1)}, bf16[8,1024]{1,0:T(8,128)(2,1)S(1)}, u32[]{:S(2)}, u32[]{:S(2)}) collective-permute-start(bf16[8,1024]{1,0:T(8,128)(2,1)S(1)} %get-tuple-element.11), channel_id=1, source_target_pairs={{0,2},{1,3},{2,0},{3,1},{4,6},{5,7},{6,4},{7,5},{8,10},{9,11},{10,... | collective-permute-start | bytes 49160 | tf_op jit(solution)/shard_map/ppermute | solution.py:13
  28.8 2.8 %collective-permute-start.8 = (bf16[8,1024]{1,0:T(8,128)(2,1)S(1)}, bf16[8,1024]{1,0:T(8,128)(2,1)S(1)}, u32[]{:S(2)}, u32[]{:S(2)}) collective-permute-start(bf16[8,1024]{1,0:T(8,128)(2,1)S(1)} %get-tuple-element.11), channel_id=1, source_target_pairs={{0,1},{1,0},{2,3},{3,2},{4,5},{5,4},{6,7},{7,6},{8,9},{9,8},{10,11... | collective-permute-start | bytes 49160 | tf_op jit(solution)/shard_map/ppermute | solution.py:13
  33.7 16.6 %copy-start.10 = (s32[2]{0:T(128)S(1)}, s32[2]{0:T(128)}, u32[]{:S(2)}) copy-start(s32[2]{0:T(128)} %param.39) | copy-start | bytes 28
  33.7 6.7 %collective-permute-start.11 = (bf16[32,1024]{1,0:T(8,128)(2,1)S(1)}, bf16[32,1024]{1,0:T(8,128)(2,1)S(1)}, u32[]{:S(2)}, u32[]{:S(2)}) collective-permute-start(bf16[32,1024]{1,0:T(8,128)(2,1)S(1)} %get-tuple-element.53), channel_id=1, source_target_pairs={{0,12},{4,8},{8,4},{12,0},{1,13},{5,9},{9,5},{13,1},{2,14},{6,10},... | collective-permute-start | bytes 196616 | tf_op jit(solution)/shard_map/ppermute | solution.py:13
  35.5 6.8 %collective-permute-start.10 = (bf16[32,1024]{1,0:T(8,128)(2,1)S(1)}, bf16[32,1024]{1,0:T(8,128)(2,1)S(1)}, u32[]{:S(2)}, u32[]{:S(2)}) collective-permute-start(bf16[32,1024]{1,0:T(8,128)(2,1)S(1)} %get-tuple-element.53), channel_id=1, source_target_pairs={{0,8},{4,12},{8,0},{12,4},{1,9},{5,13},{9,1},{13,5},{2,10},{6,14},... | collective-permute-start | bytes 196616 | tf_op jit(solution)/shard_map/ppermute | solution.py:13
  35.9 6.4 %collective-permute-start.9 = (bf16[32,1024]{1,0:T(8,128)(2,1)S(1)}, bf16[32,1024]{1,0:T(8,128)(2,1)S(1)}, u32[]{:S(2)}, u32[]{:S(2)}) collective-permute-start(bf16[32,1024]{1,0:T(8,128)(2,1)S(1)} %get-tuple-element.53), channel_id=1, source_target_pairs={{0,4},{4,0},{8,12},{12,8},{1,5},{5,1},{9,13},{13,9},{2,6},{6,2},{1... | collective-permute-start | bytes 196616 | tf_op jit(solution)/shard_map/ppermute | solution.py:13
  46.7 10.7 %all-to-all-start = ((bf16[16,2,1280]{2,1,0:T(2,128)(2,1)}), bf16[16,2,1280]{2,1,0:T(2,128)(2,1)S(1)}, u32[]{:S(2)}, u32[]{:S(2)}) async-start(bf16[16,2,1280]{2,1,0:T(2,128)(2,1)} %concatenate.50), calls=%async_computation | async-start | bytes 163840 | tf_op jit(solution)/shard_map/all_to_all | solution.py:145
  70.0 32.0 %collective-permute-start.14 = (bf16[32,1024]{1,0:T(8,128)(2,1)S(1)}, bf16[32,1024]{1,0:T(8,128)(2,1)S(1)}, u32[]{:S(2)}, u32[]{:S(2)}) collective-permute-start(bf16[32,1024]{1,0:T(8,128)(2,1)S(1)} %get-tuple-element.57), channel_id=1, source_target_pairs={{0,12},{4,8},{8,4},{12,0},{1,13},{5,9},{9,5},{13,1},{2,14},{6,10},... | collective-permute-start | bytes 196616 | tf_op jit(solution)/shard_map/ppermute | solution.py:13
  70.5 31.5 %collective-permute-start.13 = (bf16[32,1024]{1,0:T(8,128)(2,1)S(1)}, bf16[32,1024]{1,0:T(8,128)(2,1)S(1)}, u32[]{:S(2)}, u32[]{:S(2)}) collective-permute-start(bf16[32,1024]{1,0:T(8,128)(2,1)S(1)} %get-tuple-element.57), channel_id=1, source_target_pairs={{0,8},{4,12},{8,0},{12,4},{1,9},{5,13},{9,1},{13,5},{2,10},{6,14},... | collective-permute-start | bytes 196616 | tf_op jit(solution)/shard_map/ppermute | solution.py:13
  71.6 30.4 %collective-permute-start.12 = (bf16[32,1024]{1,0:T(8,128)(2,1)S(1)}, bf16[32,1024]{1,0:T(8,128)(2,1)S(1)}, u32[]{:S(2)}, u32[]{:S(2)}) collective-permute-start(bf16[32,1024]{1,0:T(8,128)(2,1)S(1)} %get-tuple-element.57), channel_id=1, source_target_pairs={{0,4},{4,0},{8,12},{12,8},{1,5},{5,1},{9,13},{13,9},{2,6},{6,2},{1... | collective-permute-start | bytes 196616 | tf_op jit(solution)/shard_map/ppermute | solution.py:13
  109.4 1.5 %collective-permute-start.15 = (bf16[32,3200]{1,0:T(8,128)(2,1)S(1)}, bf16[32,3200]{1,0:T(8,128)(2,1)S(1)}, u32[]{:S(2)}, u32[]{:S(2)}) collective-permute-start(bf16[32,3200]{1,0:T(8,128)(2,1)S(1)} %concatenate.54), channel_id=1, source_target_pairs={{0,1},{1,0},{2,3},{3,2},{4,5},{5,4},{6,7},{7,6},{8,9},{9,8},{10,11... | collective-permute-start | bytes 614408 | tf_op jit(solution)/shard_map/ppermute | solution.py:13
  111.4 7.2 %collective-permute-start.16 = (bf16[32,3200]{1,0:T(8,128)(2,1)S(1)}, bf16[32,3200]{1,0:T(8,128)(2,1)S(1)}, u32[]{:S(2)}, u32[]{:S(2)}) collective-permute-start(bf16[32,3200]{1,0:T(8,128)(2,1)S(1)} %convert_element_type.199), channel_id=1, source_target_pairs={{0,2},{1,3},{2,0},{3,1},{4,6},{5,7},{6,4},{7,5},{8,10},{9,11},{10,... | collective-permute-start | bytes 614408 | tf_op jit(solution)/shard_map/ppermute | solution.py:13
  119.0 1.4 %collective-permute-start.17 = (bf16[32,1536]{1,0:T(8,128)(2,1)S(1)}, bf16[32,1536]{1,0:T(8,128)(2,1)S(1)}, u32[]{:S(2)}, u32[]{:S(2)}) collective-permute-start(bf16[32,1536]{1,0:T(8,128)(2,1)S(1)} %fusion.18), channel_id=1, source_target_pairs={{0,1},{1,0},{2,3},{3,2},{4,5},{5,4},{6,7},{7,6},{8,9},{9,8},{10,11... | collective-permute-start | bytes 294920 | tf_op jit(solution)/shard_map/ppermute | solution.py:13
  124.7 5.6 %collective-permute-start.20 = (bf16[8,1024]{1,0:T(8,128)(2,1)S(1)}, bf16[8,1024]{1,0:T(8,128)(2,1)S(1)}, u32[]{:S(2)}, u32[]{:S(2)}) collective-permute-start(bf16[8,1024]{1,0:T(8,128)(2,1)S(1)} %get-tuple-element.23), channel_id=1, source_target_pairs={{0,12},{4,8},{8,4},{12,0},{1,13},{5,9},{9,5},{13,1},{2,14},{6,10},... | collective-permute-start | bytes 49160 | tf_op jit(solution)/shard_map/ppermute | solution.py:13
  125.3 5.0 %collective-permute-start.19 = (bf16[8,1024]{1,0:T(8,128)(2,1)S(1)}, bf16[8,1024]{1,0:T(8,128)(2,1)S(1)}, u32[]{:S(2)}, u32[]{:S(2)}) collective-permute-start(bf16[8,1024]{1,0:T(8,128)(2,1)S(1)} %get-tuple-element.24), channel_id=1, source_target_pairs={{0,8},{4,12},{8,0},{12,4},{1,9},{5,13},{9,1},{13,5},{2,10},{6,14},... | collective-permute-start | bytes 49160 | tf_op jit(solution)/shard_map/ppermute | solution.py:13
  126.2 4.6 %collective-permute-start.18 = (bf16[8,1024]{1,0:T(8,128)(2,1)S(1)}, bf16[8,1024]{1,0:T(8,128)(2,1)S(1)}, u32[]{:S(2)}, u32[]{:S(2)}) collective-permute-start(bf16[8,1024]{1,0:T(8,128)(2,1)S(1)} %get-tuple-element.22), channel_id=1, source_target_pairs={{0,4},{4,0},{8,12},{12,8},{1,5},{5,1},{9,13},{13,9},{2,6},{6,2},{1... | collective-permute-start | bytes 49160 | tf_op jit(solution)/shard_map/ppermute | solution.py:13
  (10 other events, 90.7 us)

commit v2 on v0

v2 whole, which is shorter than its diff:
```python
import functools

import jax
import jax.numpy as jnp
from jax import lax
from jax.experimental import pallas as pl
from jax.experimental.pallas import tpu as pltpu
from jax.sharding import PartitionSpec as P

EPS = 1e-06
F32 = jnp.float32
BF16 = jnp.bfloat16
LANES = 128
MIB = 1024 * 1024


def swap(value, axis, mask):
    return lax.ppermute(value, axis, [(i, i ^ mask) for i in range(lax.axis_size(axis))])


def on_chip(weight):
    return pltpu.with_memory_space_constraint(weight, pltpu.VMEM)


def shape(dims, dtype):
    return jax.ShapeDtypeStruct(dims, dtype)


def call(kernel, name, outs, scalars, arrays, scratch=(), grant=6):
    work = sum(a.size * a.dtype.itemsize for a in arrays)
    return pl.pallas_call(
        kernel,
        out_shape=outs,
        in_specs=[pl.BlockSpec(memory_space=pltpu.SMEM)] * len(scalars)
        + [pl.BlockSpec(memory_space=pltpu.VMEM)] * len(arrays),
        out_specs=[pl.BlockSpec(memory_space=pltpu.VMEM)] * len(outs),
        scratch_shapes=list(scratch),
        compiler_params=pltpu.CompilerParams(vmem_limit_bytes=grant * MIB),
        cost_estimate=pl.CostEstimate(flops=32 * work, bytes_accessed=work, transcendentals=0),
        name=name,
    )(*scalars, *arrays)


def dot(a, b):
    return jnp.dot(a, b, preferred_element_type=F32)


def product(normed, weight, write, width=512):
    columns = weight.shape[-1]
    step = width if columns % width == 0 else columns
    for at in range(0, columns, step):
        write(at, step, dot(normed, weight[:, at : at + step]))


def square_lanes(squares):
    high = squares.astype(BF16).astype(F32)
    low = squares - high
    lane = lax.broadcasted_iota(jnp.int32, (squares.shape[0], LANES), 1)
    return jnp.where(lane < LANES // 2, high, low)


def factor_of(lanes, features):
    squares = lanes[:, :1] + lanes[:, LANES // 2 : LANES // 2 + 1]
    return lax.rsqrt(squares / features + EPS)


def sum_squares(stream):
    return jnp.sum(stream * stream, axis=1, keepdims=True)


def gelu(v):
    return 0.5 * v * (1.0 + jnp.tanh(0.7978845608028654 * (v + 0.044715 * (v * v * v))))


def sigmoid(v):
    return 1.0 / (1.0 + jnp.exp(-v))


def rows_of(block, size):
    return pl.ds(pl.multiple_of(block * size, size), size)


def rec_in_kernel(nr, nc, at_ref, *refs):
    blocks, refs = refs[:nr], refs[nr:]
    gain, weight, tokens_all, keep = refs[:4]
    lows, (stream, part) = refs[4 : 3 + nc], refs[3 + nc :]
    row, col = at_ref[0], at_ref[1]
    size = blocks[0].shape[0]
    for m in range(nr):
        stream[rows_of(row ^ m, size), :] = blocks[m][...].astype(F32)
    value = stream[...]
    tokens_all[...] = value.astype(BF16)
    here = weight.shape[2]
    part[:, 2 * here :] = square_lanes(sum_squares(value))
    normed = (value * gain[...].astype(F32)).astype(BF16)
    for g in range(2):

        def write(at, step, result):
            part[:, g * here + at : g * here + at + step] = result

        product(normed, weight.at[g], write)
    size = keep.shape[0]
    for m in range(1, nc):
        lows[m - 1][...] = part[rows_of(col ^ m, size), :].astype(BF16)
    keep[...] = part[rows_of(col, size), :]


def recurrent_kernel(nc, features, *refs):
    keep, lows, refs = refs[0], refs[1:nc], refs[nc:]
    taps, bias, conv_state, gate_weight, gate_bias, lru_param, lru_state, state_ref, mixed_ref = refs
    here = lru_state.shape[1]
    total = keep[...]
    for low in lows:
        total = total + low[...].astype(F32)
    factor = factor_of(total[:, 2 * here :], features)
    convolved = taps[0:1, :].astype(F32) * (total[:, :here] * factor) + bias[...].astype(F32)
    for offset in range(conv_state.shape[0]):
        convolved = convolved + taps[offset + 1 : offset + 2, :].astype(F32) * conv_state[
            offset
        ].astype(F32)
    conv_low = convolved.astype(BF16)
    size = gate_weight.shape[2]
    for h in range(gate_weight.shape[1]):
        cut = slice(h * size, (h + 1) * size)
        decay_gate = dot(conv_low[:, cut], gate_weight[0, h]) + gate_bias[0:1, cut].astype(F32)
        input_gate = dot(conv_low[:, cut], gate_weight[1, h]) + gate_bias[1:2, cut].astype(F32)
        softplus = jnp.log(1.0 + jnp.exp(lru_param[:, cut]))
        log_decay = -8.0 * sigmoid(decay_gate) * softplus
        state = jnp.exp(log_decay) * lru_state[:, cut] + jnp.sqrt(
            1.0 - jnp.exp(2.0 * log_decay)
        ) * (sigmoid(input_gate) * convolved[:, cut])
        state_ref[:, cut] = state
        branch_y = total[:, here + h * size : here + (h + 1) * size] * factor
        mixed_ref[:, cut] = (state * gelu(branch_y)).astype(BF16)


def rec_out_kernel(nc, at_ref, *refs):
    blocks, (weight, low, mixed) = refs[:nc], refs[nc:]
    size = blocks[0].shape[0]
    for m in range(nc):
        mixed[rows_of(at_ref[1] ^ m, size), :] = blocks[m][...].astype(F32)

    def write(at, step, result):
        low[:, at : at + step] = result.astype(BF16)

    product(mixed[...].astype(BF16), weight, write)


def query_kernel(nr, *refs):
    stream, lows, refs = refs[0], refs[1 : 1 + nr], refs[1 + nr :]
    gain, query_weight, kv_slice, stream_out, sent, part = refs
    value = stream[...].astype(F32)
    for low in lows:
        value = value + low[...].astype(F32)
    stream_out[...] = value
    heads = query_weight.shape[1]
    part[:, heads : heads + LANES] = square_lanes(sum_squares(value))
    normed = (value * gain[...].astype(F32)).astype(BF16)

    def write(at, step, result):
        part[:, at : at + step] = result

    product(normed, query_weight, write)
    part[:, heads + LANES :] = dot(normed, kv_slice[...])
    size = sent.shape[1]
    for block in range(sent.shape[0]):
        sent[block] = part[block * size : (block + 1) * size, :].astype(BF16)


def turn(v, cosine, sine):
    half = cosine.shape[1]
    first, second = v[:, :half], v[:, half:]
    return jnp.concatenate(
        [first * cosine - second * sine, second * cosine + first * sine], axis=1
    )


def attention_kernel(nr, nc, features, lengths, slots, *refs):
    arrived, cosine_ref, sine_ref, keys, values, sent, entries, query, attended, kv = refs
    owners, window, head_dim = keys.shape
    cosine, sine = cosine_ref[...], sine_ref[...]
    heads_here = sent.shape[2]
    group = heads_here // head_dim
    kv_here = kv.shape[1] // nr
    scale = head_dim ** (-0.5)
    factor = None
    for r in range(nr):
        total = jnp.sum(arrived[r * nc : (r + 1) * nc].astype(F32), axis=0)
        if factor is None:
            factor = factor_of(total[:, heads_here : heads_here + LANES], features)
        kv[:, r * kv_here : (r + 1) * kv_here] = total[:, heads_here + LANES :] * factor
        low = (total[:, :heads_here] * factor).astype(BF16).astype(F32)
        for h in range(group):
            turned = turn(low[:, h * head_dim : (h + 1) * head_dim], cosine, sine) * scale
            for b in range(owners):
                query[b, r * group + h : r * group + h + 1, :] = turned[b : b + 1, :]
    key_new = turn(kv[:, :head_dim], cosine, sine).astype(BF16)
    value_new = kv[:, head_dim:].astype(BF16)
    entries[:, :head_dim] = key_new
    entries[:, head_dim:] = value_new
    slot_index = lax.broadcasted_iota(jnp.int32, (1, window), 1)
    for b in range(owners):
        q = query[b].astype(BF16)
        scores = lax.dot_general(
            q, keys[b], (((1,), (1,)), ((), ())), preferred_element_type=F32
        )
        self_score = jnp.sum(
            q.astype(F32) * key_new[b : b + 1, :].astype(F32), axis=1, keepdims=True
        )
        age = slots[b] - slot_index
        age = jnp.where(age < 0, age + window, age)
        valid = (age >= 1) & (age <= lengths[b])
        masked = jnp.where(valid, scores, -1e30)
        top = jnp.maximum(jnp.max(masked, axis=1, keepdims=True), self_score)
        weights = jnp.exp(masked - top)
        self_weight = jnp.exp(self_score - top)
        total = jnp.sum(weights, axis=1, keepdims=True) + self_weight
        result = dot((weights / total).astype(BF16), values[b])
        self_low = (self_weight / total).astype(BF16).astype(F32)
        result = result + self_low * value_new[b : b + 1, :].astype(F32)
        for h in range(nr * group):
            attended[b : b + 1, h * head_dim : (h + 1) * head_dim] = result[h : h + 1, :]
    for r in range(nr):
        low = attended[:, r * heads_here : (r + 1) * heads_here].astype(BF16)
        for c in range(nc):
            sent[r * nc + c] = low


def attn_out_kernel(arrived, weight, low, rows):
    size = arrived.shape[1]
    for block in range(arrived.shape[0]):
        rows[block * size : (block + 1) * size, :] = arrived[block].astype(F32)

    def write(at, step, result):
        low[:, at : at + step] = result.astype(BF16)

    product(rows[...].astype(BF16), weight, write)


def mlp_in_kernel(nr, cores, at_ref, *refs):
    stream, lows, refs = refs[0], refs[1 : 1 + nr], refs[1 + nr :]
    gain, weight, stream_out, keep = refs[:4]
    value = stream[...]
    for low in lows:
        value = value + low[...].astype(F32)
    stream_out[...] = value
    normed = (value * gain[...].astype(F32)).astype(BF16)
    lanes = square_lanes(sum_squares(value))
    here = weight.shape[2] // cores
    core = at_ref[1] % cores
    for m in reversed(range(cores)):
        out = refs[3 + m]
        out[:, 2 * here :] = lanes.astype(out.dtype)
        start = (core ^ m) * here
        step = 512 if here % 512 == 0 else here
        for g in range(2):
            for at in range(0, here, step):
                cut = pl.ds(pl.multiple_of(start + at, LANES), step)
                out[:, g * here + at : g * here + at + step] = dot(
                    normed, weight[g, :, cut]
                ).astype(out.dtype)


def pair_kernel(keep, arrived, low):
    wide = low.shape[1] - LANES
    total = keep[...] + arrived[...].astype(F32)
    low[:, :wide] = total[:, :wide].astype(BF16)
    squares = total[:, wide : wide + 1] + total[:, wide + LANES // 2 : wide + LANES // 2 + 1]
    low[:, wide:] = square_lanes(squares).astype(BF16)


def hidden_kernel(features, *refs):
    lows, hidden = refs[:-1], refs[-1]
    here = hidden.shape[1]
    total = lows[0][...].astype(F32)
    for low in lows[1:]:
        total = total + low[...].astype(F32)
    factor = factor_of(total[:, 2 * here :], features)
    hidden[...] = (gelu(total[:, :here] * factor) * (total[:, here : 2 * here] * factor)).astype(
        BF16
    )


def mlp_out_kernel(nr, cores, at_ref, *refs):
    hiddens, refs = refs[:cores], refs[cores:]
    stream, weight, keep = refs[:3]
    lows, part = refs[3 : 2 + nr], refs[2 + nr]
    here = hiddens[0].shape[1]
    core, row = at_ref[1] % cores, at_ref[0]
    columns = weight.shape[1]
    step = 512 if columns % 512 == 0 else columns
    for at in range(0, columns, step):
        total = None
        for m in range(cores):
            cut = pl.ds(pl.multiple_of((core ^ m) * here, LANES), here)
            result = dot(hiddens[m][...], weight[cut, at : at + step])
            total = result if total is None else total + result
        part[:, at : at + step] = total
    size = keep.shape[0]
    for m in range(1, nr):
        lows[m - 1][...] = part[rows_of(row ^ m, size), :].astype(BF16)
    own = rows_of(row, size)
    keep[...] = part[own, :] + stream[own, :]


def result_kernel(*refs):
    total = refs[0][...]
    for low in refs[1:-1]:
        total = total + low[...].astype(F32)
    refs[-1][...] = total.astype(BF16)


def per_device(
    tokens,
    rec_gain,
    rec_in_weight,
    conv_weight,
    conv_bias,
    conv_state,
    gate_weight,
    gate_bias,
    lru_param,
    lru_state,
    rec_out_weight,
    attn_gain,
    query_weight,
    kv_weight,
    key_cache,
    value_cache,
    lengths,
    write_slots,
    attn_out_weight,
    mlp_gain,
    mlp_in_weight,
    mlp_out_weight,
):
    nr = lax.axis_size("req")
    nc = lax.axis_size("chan")
    at = jnp.stack([lax.axis_index("req"), lax.axis_index("chan")]).astype(jnp.int32)
    local_rows, local_features = tokens.shape
    rows = local_rows * nr
    features = local_features * nc
    lru_rows, lru_here = lru_state.shape
    blocks = [tokens] + [swap(tokens, "req", m) for m in range(1, nr)]
    wide = 2 * lru_here + LANES
    tokens_all, keep, *lows = call(
        functools.partial(rec_in_kernel, nr, nc),
        "rec_in",
        [shape((rows, local_features), BF16), shape((lru_rows, wide), F32)]
        + [shape((lru_rows, wide), BF16)] * (nc - 1),
        [at],
        blocks + [rec_gain[None, :], on_chip(rec_in_weight)],
        [pltpu.VMEM((rows, local_features), F32), pltpu.VMEM((rows, wide), F32)],
    )
    lows = [swap(low, "chan", m + 1) for m, low in enumerate(lows)]
    new_state, mixed = call(
        functools.partial(recurrent_kernel, nc, features),
        "recurrent",
        [shape((lru_rows, lru_here), F32), shape((lru_rows, lru_here), BF16)],
        [],
        [keep]
        + lows
        + [
            conv_weight,
            conv_bias[None, :],
            conv_state,
            on_chip(gate_weight),
            gate_bias,
            lru_param[None, :],
            lru_state,
        ],
    )
    (low,) = call(
        functools.partial(rec_out_kernel, nc),
        "rec_out",
        [shape((rows, local_features), BF16)],
        [at],
        [mixed] + [swap(mixed, "chan", m) for m in range(1, nc)] + [on_chip(rec_out_weight)],
        [pltpu.VMEM((rows, lru_here), F32)],
    )
    lows = [low] + [swap(low, "req", m) for m in range(1, nr)]
    kv_here = kv_weight.shape[1] // nr
    kv_slice = lax.dynamic_slice_in_dim(kv_weight, at[0] * kv_here, kv_here, 1)
    owners = rows // (nr * nc)
    heads_here = query_weight.shape[1]
    wide = heads_here + LANES + kv_here
    stream, sent = call(
        functools.partial(query_kernel, nr),
        "query",
        [shape((rows, local_features), F32), shape((nr * nc, owners, wide), BF16)],
        [],
        [tokens_all] + lows + [attn_gain[None, :], on_chip(query_weight), kv_slice],
        [pltpu.VMEM((rows, wide), F32)],
    )
    arrived = lax.all_to_all(sent, ("req", "chan"), split_axis=0, concat_axis=0, tiled=True)
    head_dim = key_cache.shape[2]
    freq = 10000.0 ** (-jnp.arange(head_dim // 2, dtype=F32) / (head_dim // 2))
    angle = lengths.astype(F32)[:, None] * freq
    sent, new_entries = call(
        functools.partial(attention_kernel, nr, nc, features),
        "attention",
        [shape((nr * nc, owners, heads_here), BF16), shape((owners, 2 * head_dim), BF16)],
        [lengths, write_slots],
        [arrived, jnp.cos(angle), jnp.sin(angle), on_chip(key_cache), on_chip(value_cache)],
        [
            pltpu.VMEM((owners, nr * heads_here // head_dim, head_dim), F32),
            pltpu.VMEM((owners, nr * heads_here), F32),
            pltpu.VMEM((owners, 2 * head_dim), F32),
        ],
    )
    arrived = lax.all_to_all(sent, ("req", "chan"), split_axis=0, concat_axis=0, tiled=True)
    (low,) = call(
        attn_out_kernel,
        "attn_out",
        [shape((rows, local_features), BF16)],
        [],
        [arrived, on_chip(attn_out_weight)],
        [pltpu.VMEM((rows, heads_here), F32)],
    )
    lows = [low] + [swap(low, "req", m) for m in range(1, nr)]
    cores = 2 if nc % 2 == 0 else 1
    hidden_here = mlp_in_weight.shape[2] // cores
    wide = 2 * hidden_here + LANES
    stream, keep, *lows = call(
        functools.partial(mlp_in_kernel, nr, cores),
        "mlp_in",
        [shape((rows, local_features), F32), shape((rows, wide), F32)]
        + [shape((rows, wide), BF16)] * (cores - 1),
        [at],
        [stream] + lows + [mlp_gain[None, :], on_chip(mlp_in_weight)],
    )
    if cores == 2:
        (low,) = call(
            pair_kernel,
            "pair",
            [shape((rows, wide), BF16)],
            [],
            [keep, swap(lows[0], "chan", 1)],
        )
    else:
        low = keep.astype(BF16)
    (hidden,) = call(
        functools.partial(hidden_kernel, features),
        "hidden",
        [shape((rows, hidden_here), BF16)],
        [],
        [low] + [swap(low, "chan", m) for m in range(cores, nc, cores)],
    )
    keep, *lows = call(
        functools.partial(mlp_out_kernel, nr, cores),
        "mlp_out",
        [shape((local_rows, local_features), F32)]
        + [shape((local_rows, local_features), BF16)] * (nr - 1),
        [at],
        [hidden]
        + [swap(hidden, "chan", m) for m in range(1, cores)]
        + [stream, on_chip(mlp_out_weight)],
        [pltpu.VMEM((rows, local_features), F32)],
    )
    (result,) = call(
        result_kernel,
        "result",
        [shape((local_rows, local_features), BF16)],
        [],
        [keep] + [swap(low, "req", m + 1) for m, low in enumerate(lows)],
    )
    return (result, new_state, new_entries)


def solution(mesh):
    return jax.shard_map(
        per_device,
        mesh=mesh,
        in_specs=(
            P(("grp", "req"), "chan"),
            P("chan"),
            P(None, "chan", "req"),
            P(None, "req"),
            P("req"),
            P(None, ("grp", "chan"), "req"),
            P(None, "req", None, None),
            P(None, "req"),
            P("req"),
            P(("grp", "chan"), "req"),
            P("req", "chan"),
            P("chan"),
            P("chan", "req"),
            P("chan", None),
            P(("grp", "req", "chan"), None, None),
            P(("grp", "req", "chan"), None, None),
            P(("grp", "req", "chan")),
            P(("grp", "req", "chan")),
            P("req", "chan"),
            P("chan"),
            P(None, "chan", "req"),
            P("req", "chan"),
        ),
        out_specs=(
            P(("grp", "req"), "chan"),
            P(("grp", "chan"), "req"),
            P(("grp", "req", "chan"), None),
        ),
        check_vma=False,
    )
```

time: 256 us -> 104 us (0.41)
  blocking collectives: 93.6 us -> 9.48 us
  waiting for transfers between devices: 104 us -> 36.4 us
  matrix products: 24.8 us -> 0 us
  starting transfers between devices: 3.72 us -> 27.3 us
  Pallas kernels: 0 us -> 13.7 us
  between operations: 14.2 us -> 0.83 us
  local copies, waits for them, and re-layouts: 4.22 us -> 15.5 us
  other arithmetic: 10.2 us -> 0.2 us
    reduce_scatter x5 -> x0, waiting for transfers between devices: 96.9 us -> none  [the longest x3 55.2 us: return_rows(): lax.psum_scatter(partial_value, 'req', scatter_dimension=0, tiled=True)]
    all_gather x6 -> x0, blocking collectives: 55.8 us -> none  [the longest x3 39.8 us: per_device(): lax.all_gather(normed, 'req', axis=0, tiled=True)]
    ppermute x0 -> x21, waiting for transfers between devices: none -> 29.4 us  [swap(): lax.ppermute(value, axis, [(i, i ^ mask) for i in range(lax.axis_size(axi...]
    dot_general x11 -> x0, matrix products: 24.8 us -> none  [the longest x2 11.5 us: per_device(): jnp.einsum('rd,gdo->gro', lax.all_gather(normed, 'req', axis=0, tiled=Tru...]
    ppermute x0 -> x21, starting transfers between devices: none -> 23.4 us  [swap(): lax.ppermute(value, axis, [(i, i ^ mask) for i in range(lax.axis_size(axi...]
    psum x3 -> x0, blocking collectives: 19.7 us -> none  [norm_rows(): summed = lax.psum(partial_value, 'chan')]
    pallas_call x0 -> x11, Pallas kernels: none -> 13.7 us  [call(): pl.pallas_call(kernel, out_shape=outs, in_specs=[pl.BlockSpec(memory_spac...]
    unnamed x35 -> x42, local copies, waits for them, and re-layouts: 1.15 us -> 14.7 us
  transfers between devices with their start and end apart: 6 -> 22, of which waited for: 6 -> 16; matrix products, arithmetic and copies ran while one was open for 1% -> 1% of each run, Pallas kernels for 0% -> 0%
where the time goes in v2:
time: 104 us; the launch traced here: 103 us
  waiting for transfers between devices  36.4 us (35%)
  starting transfers between devices  27.3 us (26%)
  local copies, waits for them, and re-layouts  15.5 us (15%)
  Pallas kernels  13.7 us (13%)
  blocking collectives  9.48 us (9%)
    ppermute x21, waiting for transfers between devices, swap(): lax.ppermute(value, axis, [(i, i ^ mask) for i in range(lax.axis_size(axi...  29.4 us
    ppermute x21, starting transfers between devices, swap(): lax.ppermute(value, axis, [(i, i ^ mask) for i in range(lax.axis_size(axi...  23.4 us
    unnamed x42, local copies, waits for them, and re-layouts  14.7 us
    pallas_call x11, Pallas kernels, call(): pl.pallas_call(kernel, out_shape=outs, in_specs=[pl.BlockSpec(memory_spac...  13.7 us
    all_to_all x1, blocking collectives, per_device(): lax.all_to_all(sent, ('req', 'chan'), split_axis=0, concat_axis=0, tiled=...  9.48 us
    all_to_all x1, waiting for transfers between devices, per_device(): lax.all_to_all(sent, ('req', 'chan'), split_axis=0, concat_axis=0, tiled=...  7 us
    all_to_all x1, starting transfers between devices, per_device(): lax.all_to_all(sent, ('req', 'chan'), split_axis=0, concat_axis=0, tiled=...  3.82 us
  transfers between devices with their start and end apart: 22, of which 16 were waited for; matrix products, arithmetic and copies ran while one was open for 1% of the time, Pallas kernels for 0%

profile of v2, /device:TPU:0, one launch (start us, length us, event | category | flops | bytes accessed | tf_op | source)
XLA Modules:
  0.0 103.4 jit_solution(4855623654379103221)
XLA Ops:
  0.6 4.1 %collective-permute-start.1 = (bf16[8,1024]{1,0:T(8,128)(2,1)}, bf16[8,1024]{1,0:T(8,128)(2,1)S(1)}, u32[]{:S(2)}, u32[]{:S(2)}) collective-permute-start(bf16[8,1024]{1,0:T(8,128)(2,1)} %refs_0_.1), channel_id=1, source_target_pairs={{0,8},{4,12},{8,0},{12,4},{1,9},{5,13},{9,1},{13,5},{2,10},{6,14},... | collective-permute-start | bytes 49160 | tf_op jit(solution)/shard_map/ppermute | solution.py:18
  4.8 1.6 %collective-permute-start = (bf16[8,1024]{1,0:T(8,128)(2,1)}, bf16[8,1024]{1,0:T(8,128)(2,1)S(1)}, u32[]{:S(2)}, u32[]{:S(2)}) collective-permute-start(bf16[8,1024]{1,0:T(8,128)(2,1)} %refs_0_.1), channel_id=1, source_target_pairs={{0,4},{4,0},{8,12},{12,8},{1,5},{5,1},{9,13},{13,9},{2,6},{6,2},{1... | collective-permute-start | bytes 49160 | tf_op jit(solution)/shard_map/ppermute | solution.py:18
  7.1 1.6 %collective-permute-done.refs_1_ = bf16[8,1024]{1,0:T(8,128)(2,1)S(1)} collective-permute-done((bf16[8,1024]{1,0:T(8,128)(2,1)}, bf16[8,1024]{1,0:T(8,128)(2,1)S(1)}, u32[]{:S(2)}, u32[]{:S(2)}) %collective-permute-start) | collective-permute-done | bytes 16416 | tf_op jit(solution)/shard_map/ppermute | solution.py:18
  8.7 3.4 %collective-permute-done.2.refs_3_ = bf16[8,1024]{1,0:T(8,128)(2,1)S(1)} collective-permute-done((bf16[8,1024]{1,0:T(8,128)(2,1)}, bf16[8,1024]{1,0:T(8,128)(2,1)S(1)}, u32[]{:S(2)}, u32[]{:S(2)}) %collective-permute-start.2) | collective-permute-done | bytes 16416 | tf_op jit(solution)/shard_map/ppermute | solution.py:18
  12.1 2.2 %copy-done.3 = bf16[2,1024,1024]{2,1,0:T(8,128)(2,1)S(1)} copy-done((bf16[2,1024,1024]{2,1,0:T(8,128)(2,1)S(1)}, bf16[2,1024,1024]{2,1,0:T(8,128)(2,1)}, u32[]{:S(2)}) %copy-start.3) | copy-done | bytes 4194328
  15.0 2.0 %rec_in.1 = (bf16[32,1024]{1,0:T(8,128)(2,1)S(1)}, f32[8,2176]{1,0:T(8,128)S(1)}, bf16[8,2176]{1,0:T(8,128)(2,1)}, bf16[8,2176]{1,0:T(8,128)(2,1)}, bf16[8,2176]{1,0:T(8,128)(2,1)S(1)}) custom-call(s32[2]{0:T(128)S(1)} %pad_add_fusion.at_ref, bf16[8,1024]{1,0:T(8,128)(2,1)S(1)} %copy-done.12, bf16[8,1024]{1,0:T(8,128)(2,1)S(1)} %collective-permute-done.refs_1_, ...), custom_call_target="tpu_custom_call" | custom-call | flops 136380416 | bytes 4261888 | tf_op jit(solution)/shard_map/rec_in/pallas_call | solution.py:31
  19.0 2.3 %collective-permute-done.4.refs_2_ = bf16[8,2176]{1,0:T(8,128)(2,1)S(1)} collective-permute-done((bf16[8,2176]{1,0:T(8,128)(2,1)}, bf16[8,2176]{1,0:T(8,128)(2,1)S(1)}, u32[]{:S(2)}, u32[]{:S(2)}) %collective-permute-start.4) | collective-permute-done | bytes 34848 | tf_op jit(solution)/shard_map/ppermute | solution.py:18
  30.1 4.2 %collective-permute-start.9 = (bf16[32,1024]{1,0:T(8,128)(2,1)S(1)}, bf16[32,1024]{1,0:T(8,128)(2,1)S(1)}, u32[]{:S(2)}, u32[]{:S(2)}) collective-permute-start(bf16[32,1024]{1,0:T(8,128)(2,1)S(1)} %rec_out.1.refs_1_), channel_id=1, source_target_pairs={{0,4},{4,0},{8,12},{12,8},{1,5},{5,1},{9,13},{13,9},{2,6},{6,2},{1... | collective-permute-start | bytes 196616 | tf_op jit(solution)/shard_map/ppermute | solution.py:18
  34.3 2.0 %collective-permute-done.11.refs_4_ = bf16[32,1024]{1,0:T(8,128)(2,1)S(1)} collective-permute-done((bf16[32,1024]{1,0:T(8,128)(2,1)S(1)}, bf16[32,1024]{1,0:T(8,128)(2,1)S(1)}, u32[]{:S(2)}, u32[]{:S(2)}) %collective-permute-start.11) | collective-permute-done | bytes 65568 | tf_op jit(solution)/shard_map/ppermute | solution.py:18
  38.1 3.8 %all-to-all-start = ((bf16[16,2,1280]{2,1,0:T(2,128)(2,1)}), bf16[16,2,1280]{2,1,0:T(2,128)(2,1)S(1)}, u32[]{:S(2)}, u32[]{:S(2)}) async-start(bf16[16,2,1280]{2,1,0:T(2,128)(2,1)} %get-tuple-element.28), calls=%async_computation | async-start | bytes 163840 | tf_op jit(solution)/shard_map/all_to_all | solution.py:395
  42.1 7.0 %all-to-all-done.refs_0_ = bf16[16,2,1280]{2,1,0:T(2,128)(2,1)S(1)} async-done(((bf16[16,2,1280]{2,1,0:T(2,128)(2,1)}), bf16[16,2,1280]{2,1,0:T(2,128)(2,1)S(1)}, u32[]{:S(2)}, u32[]{:S(2)}) %all-to-all-start) | async-done | bytes 81952 | tf_op jit(solution)/shard_map/all_to_all | solution.py:395
  49.1 1.6 %copy-done.6 = bf16[2,2048,256]{2,1,0:T(8,128)(2,1)S(1)} copy-done((bf16[2,2048,256]{2,1,0:T(8,128)(2,1)S(1)}, bf16[2,2048,256]{2,1,0:T(8,128)(2,1)}, u32[]{:S(2)}) %copy-start.6) | copy-done | bytes 2097176
  50.7 1.6 %copy-done.7 = bf16[2,2048,256]{2,1,0:T(8,128)(2,1)S(1)} copy-done((bf16[2,2048,256]{2,1,0:T(8,128)(2,1)S(1)}, bf16[2,2048,256]{2,1,0:T(8,128)(2,1)}, u32[]{:S(2)}) %copy-start.7) | copy-done | bytes 2097176
  52.3 2.5 %attention.1 = (bf16[16,2,1024]{2,1,0:T(2,128)(2,1)S(1)}, bf16[2,512]{1,0:T(2,128)(2,1)}) custom-call(s32[2]{0:T(128)S(1)} %copy-done.16, s32[2]{0:T(128)S(1)} %copy-done.17, bf16[16,2,1280]{2,1,0:T(2,128)(2,1)S(1)} %all-to-all-done.refs_0_, f32[2,128]{1,0:T(2,128)S(1)} %get-tuple-element.40.refs_1_, f32[2,128]{1,0:T(2,128)S(1)} %get-tuple-element.39.refs_2_, ...), custom_call_target="tpu_custom_call" | custom-call | flops 136904704 | bytes 4278272 | tf_op jit(solution)/shard_map/attention/pallas_call | solution.py:31
  54.7 9.5 %all_to_all.10.arrived = bf16[16,2,1024]{2,1,0:T(2,128)(2,1)S(1)} all-to-all(bf16[16,2,1024]{2,1,0:T(2,128)(2,1)S(1)} %get-tuple-element.29), channel_id=1, replica_groups=mesh['grp'=2,'req'=4,'chan'=4] {'req','chan'}, dimensions={0} | all-to-all | bytes 131072 | tf_op jit(solution)/shard_map/all_to_all | solution.py:411
  66.3 2.8 %collective-permute-start.12 = (bf16[32,1024]{1,0:T(8,128)(2,1)S(1)}, bf16[32,1024]{1,0:T(8,128)(2,1)S(1)}, u32[]{:S(2)}, u32[]{:S(2)}) collective-permute-start(bf16[32,1024]{1,0:T(8,128)(2,1)S(1)} %attn_out.1.refs_1_), channel_id=1, source_target_pairs={{0,4},{4,0},{8,12},{12,8},{1,5},{5,1},{9,13},{13,9},{2,6},{6,2},{1... | collective-permute-start | bytes 196616 | tf_op jit(solution)/shard_map/ppermute | solution.py:18
  69.1 2.5 %collective-permute-done.14.refs_4_ = bf16[32,1024]{1,0:T(8,128)(2,1)S(1)} collective-permute-done((bf16[32,1024]{1,0:T(8,128)(2,1)S(1)}, bf16[32,1024]{1,0:T(8,128)(2,1)S(1)}, u32[]{:S(2)}, u32[]{:S(2)}) %collective-permute-start.14) | collective-permute-done | bytes 65568 | tf_op jit(solution)/shard_map/ppermute | solution.py:18
  72.8 4.6 %copy-done.1 = bf16[2,1024,3072]{2,1,0:T(8,128)(2,1)S(1)} copy-done((bf16[2,1024,3072]{2,1,0:T(8,128)(2,1)S(1)}, bf16[2,1024,3072]{2,1,0:T(8,128)(2,1)}, u32[]{:S(2)}) %copy-start.1) | copy-done | bytes 12582936
  77.3 2.8 %mlp_in.1 = (f32[32,1024]{1,0:T(8,128)S(1)}, f32[32,3200]{1,0:T(8,128)S(1)}, bf16[32,3200]{1,0:T(8,128)(2,1)S(1)}) custom-call(s32[2]{0:T(128)S(1)} %pad_add_fusion.at_ref, f32[32,1024]{1,0:T(8,128)S(1)} %get-tuple-element.27.refs_0_, bf16[32,1024]{1,0:T(8,128)(2,1)S(1)} %attn_out.1.refs_1_, bf16[32,1024]{1,0:T(8,128)(2,1)S(1)} %collective-permute-done.12.refs_2_, ...), custom_call_target="tpu_custom_call" | custom-call | flops 415301632 | bytes 12978176 | tf_op jit(solution)/shard_map/mlp_in/pallas_call | solution.py:31
  82.5 6.5 %collective-permute-done.16.refs_1_ = bf16[32,3200]{1,0:T(8,128)(2,1)S(1)} collective-permute-done((bf16[32,3200]{1,0:T(8,128)(2,1)S(1)}, bf16[32,3200]{1,0:T(8,128)(2,1)S(1)}, u32[]{:S(2)}, u32[]{:S(2)}) %collective-permute-start.16) | collective-permute-done | bytes 204832 | tf_op jit(solution)/shard_map/ppermute | solution.py:18
  90.5 2.8 %copy-done.2 = bf16[3072,1024]{1,0:T(8,128)(2,1)S(1)} copy-done((bf16[3072,1024]{1,0:T(8,128)(2,1)S(1)}, bf16[3072,1024]{1,0:T(8,128)(2,1)}, u32[]{:S(2)}) %copy-start.2) | copy-done | bytes 6291480
  93.3 1.7 %mlp_out.1 = (f32[8,1024]{1,0:T(8,128)S(1)}, bf16[8,1024]{1,0:T(8,128)(2,1)S(1)}, bf16[8,1024]{1,0:T(8,128)(2,1)S(1)}, bf16[8,1024]{1,0:T(8,128)(2,1)S(1)}) custom-call(s32[2]{0:T(128)S(1)} %pad_add_fusion.at_ref, bf16[32,1536]{1,0:T(8,128)(2,1)S(1)} %hidden.1.refs_0_, bf16[32,1536]{1,0:T(8,128)(2,1)S(1)} %collective-permute-done.17.refs_1_, ...), custom_call_target="tpu_custom_call" | custom-call | flops 211812352 | bytes 6619136 | tf_op jit(solution)/shard_map/mlp_out/pallas_call | solution.py:31
  97.2 2.3 %collective-permute-start.20 = (bf16[8,1024]{1,0:T(8,128)(2,1)S(1)}, bf16[8,1024]{1,0:T(8,128)(2,1)S(1)}, u32[]{:S(2)}, u32[]{:S(2)}) collective-permute-start(bf16[8,1024]{1,0:T(8,128)(2,1)S(1)} %get-tuple-element.36), channel_id=1, source_target_pairs={{0,12},{4,8},{8,4},{12,0},{1,13},{5,9},{9,5},{13,1},{2,14},{6,10},... | collective-permute-start | bytes 49160 | tf_op jit(solution)/shard_map/ppermute | solution.py:18
  100.4 2.4 %collective-permute-done.20.refs_3_ = bf16[8,1024]{1,0:T(8,128)(2,1)S(1)} collective-permute-done((bf16[8,1024]{1,0:T(8,128)(2,1)S(1)}, bf16[8,1024]{1,0:T(8,128)(2,1)S(1)}, u32[]{:S(2)}, u32[]{:S(2)}) %collective-permute-start.20) | collective-permute-done | bytes 16416 | tf_op jit(solution)/shard_map/ppermute | solution.py:18
  (83 shorter events, 25.0 us)
Async XLA Ops:
  0.6 25.5 %copy-start = (bf16[1024,512]{1,0:T(8,128)(2,1)S(1)}, bf16[1024,512]{1,0:T(8,128)(2,1)}, u32[]{:S(2)}) copy-start(bf16[1024,512]{1,0:T(8,128)(2,1)} %param.35) | copy-start | bytes 3145732
  0.6 6.5 %collective-permute-start.1 = (bf16[8,1024]{1,0:T(8,128)(2,1)}, bf16[8,1024]{1,0:T(8,128)(2,1)S(1)}, u32[]{:S(2)}, u32[]{:S(2)}) collective-permute-start(bf16[8,1024]{1,0:T(8,128)(2,1)} %refs_0_.1), channel_id=1, source_target_pairs={{0,8},{4,12},{8,0},{12,4},{1,9},{5,13},{9,1},{13,5},{2,10},{6,14},... | collective-permute-start | bytes 49160 | tf_op jit(solution)/shard_map/ppermute | solution.py:18
  4.8 3.9 %collective-permute-start = (bf16[8,1024]{1,0:T(8,128)(2,1)}, bf16[8,1024]{1,0:T(8,128)(2,1)S(1)}, u32[]{:S(2)}, u32[]{:S(2)}) collective-permute-start(bf16[8,1024]{1,0:T(8,128)(2,1)} %refs_0_.1), channel_id=1, source_target_pairs={{0,4},{4,0},{8,12},{12,8},{1,5},{5,1},{9,13},{13,9},{2,6},{6,2},{1... | collective-permute-start | bytes 49160 | tf_op jit(solution)/shard_map/ppermute | solution.py:18
  6.4 5.7 %collective-permute-start.2 = (bf16[8,1024]{1,0:T(8,128)(2,1)}, bf16[8,1024]{1,0:T(8,128)(2,1)S(1)}, u32[]{:S(2)}, u32[]{:S(2)}) collective-permute-start(bf16[8,1024]{1,0:T(8,128)(2,1)} %refs_0_.1), channel_id=1, source_target_pairs={{0,12},{4,8},{8,4},{12,0},{1,13},{5,9},{9,5},{13,1},{2,14},{6,10},... | collective-permute-start | bytes 49160 | tf_op jit(solution)/shard_map/ppermute | solution.py:18
  17.1 1.9 %collective-permute-start.3 = (bf16[8,2176]{1,0:T(8,128)(2,1)}, bf16[8,2176]{1,0:T(8,128)(2,1)S(1)}, u32[]{:S(2)}, u32[]{:S(2)}) collective-permute-start(bf16[8,2176]{1,0:T(8,128)(2,1)} %get-tuple-element.23), channel_id=1, source_target_pairs={{0,1},{1,0},{2,3},{3,2},{4,5},{5,4},{6,7},{7,6},{8,9},{9,8},{10,11... | collective-permute-start | bytes 104456 | tf_op jit(solution)/shard_map/ppermute | solution.py:18
  17.1 4.1 %collective-permute-start.4 = (bf16[8,2176]{1,0:T(8,128)(2,1)}, bf16[8,2176]{1,0:T(8,128)(2,1)S(1)}, u32[]{:S(2)}, u32[]{:S(2)}) collective-permute-start(bf16[8,2176]{1,0:T(8,128)(2,1)} %get-tuple-element.24), channel_id=1, source_target_pairs={{0,2},{1,3},{2,0},{3,1},{4,6},{5,7},{6,4},{7,5},{8,10},{9,11},{10,... | collective-permute-start | bytes 104456 | tf_op jit(solution)/shard_map/ppermute | solution.py:18
  18.6 3.4 %collective-permute-start.5 = (bf16[8,2176]{1,0:T(8,128)(2,1)S(1)}, bf16[8,2176]{1,0:T(8,128)(2,1)S(1)}, u32[]{:S(2)}, u32[]{:S(2)}) collective-permute-start(bf16[8,2176]{1,0:T(8,128)(2,1)S(1)} %get-tuple-element.25), channel_id=1, source_target_pairs={{0,3},{1,2},{2,1},{3,0},{4,7},{5,6},{6,5},{7,4},{8,11},{9,10},{10,... | collective-permute-start | bytes 104456 | tf_op jit(solution)/shard_map/ppermute | solution.py:18
  24.2 3.2 %collective-permute-start.8 = (bf16[8,1024]{1,0:T(8,128)(2,1)S(1)}, bf16[8,1024]{1,0:T(8,128)(2,1)S(1)}, u32[]{:S(2)}, u32[]{:S(2)}) collective-permute-start(bf16[8,1024]{1,0:T(8,128)(2,1)S(1)} %get-tuple-element.26.refs_0_), channel_id=1, source_target_pairs={{0,3},{1,2},{2,1},{3,0},{4,7},{5,6},{6,5},{7,4},{8,11},{9,10},{10,... | collective-permute-start | bytes 49160 | tf_op jit(solution)/shard_map/ppermute | solution.py:18
  25.1 3.7 %collective-permute-start.7 = (bf16[8,1024]{1,0:T(8,128)(2,1)S(1)}, bf16[8,1024]{1,0:T(8,128)(2,1)S(1)}, u32[]{:S(2)}, u32[]{:S(2)}) collective-permute-start(bf16[8,1024]{1,0:T(8,128)(2,1)S(1)} %get-tuple-element.26.refs_0_), channel_id=1, source_target_pairs={{0,2},{1,3},{2,0},{3,1},{4,6},{5,7},{6,4},{7,5},{8,10},{9,11},{10,... | collective-permute-start | bytes 49160 | tf_op jit(solution)/shard_map/ppermute | solution.py:18
  26.1 2.8 %collective-permute-start.6 = (bf16[8,1024]{1,0:T(8,128)(2,1)S(1)}, bf16[8,1024]{1,0:T(8,128)(2,1)S(1)}, u32[]{:S(2)}, u32[]{:S(2)}) collective-permute-start(bf16[8,1024]{1,0:T(8,128)(2,1)S(1)} %get-tuple-element.26.refs_0_), channel_id=1, source_target_pairs={{0,1},{1,0},{2,3},{3,2},{4,5},{5,4},{6,7},{7,6},{8,9},{9,8},{10,11... | collective-permute-start | bytes 49160 | tf_op jit(solution)/shard_map/ppermute | solution.py:18
  26.2 22.9 %copy-start.17 = (s32[2]{0:T(128)S(1)}, s32[2]{0:T(128)}, u32[]{:S(2)}) copy-start(s32[2]{0:T(128)} %slots.1) | copy-start | bytes 28
  29.9 6.4 %collective-permute-start.11 = (bf16[32,1024]{1,0:T(8,128)(2,1)S(1)}, bf16[32,1024]{1,0:T(8,128)(2,1)S(1)}, u32[]{:S(2)}, u32[]{:S(2)}) collective-permute-start(bf16[32,1024]{1,0:T(8,128)(2,1)S(1)} %rec_out.1.refs_1_), channel_id=1, source_target_pairs={{0,12},{4,8},{8,4},{12,0},{1,13},{5,9},{9,5},{13,1},{2,14},{6,10},... | collective-permute-start | bytes 196616 | tf_op jit(solution)/shard_map/ppermute | solution.py:18
  30.1 6.2 %collective-permute-start.10 = (bf16[32,1024]{1,0:T(8,128)(2,1)S(1)}, bf16[32,1024]{1,0:T(8,128)(2,1)S(1)}, u32[]{:S(2)}, u32[]{:S(2)}) collective-permute-start(bf16[32,1024]{1,0:T(8,128)(2,1)S(1)} %rec_out.1.refs_1_), channel_id=1, source_target_pairs={{0,8},{4,12},{8,0},{12,4},{1,9},{5,13},{9,1},{13,5},{2,10},{6,14},... | collective-permute-start | bytes 196616 | tf_op jit(solution)/shard_map/ppermute | solution.py:18
  30.1 6.9 %collective-permute-start.9 = (bf16[32,1024]{1,0:T(8,128)(2,1)S(1)}, bf16[32,1024]{1,0:T(8,128)(2,1)S(1)}, u32[]{:S(2)}, u32[]{:S(2)}) collective-permute-start(bf16[32,1024]{1,0:T(8,128)(2,1)S(1)} %rec_out.1.refs_1_), channel_id=1, source_target_pairs={{0,4},{4,0},{8,12},{12,8},{1,5},{5,1},{9,13},{13,9},{2,6},{6,2},{1... | collective-permute-start | bytes 196616 | tf_op jit(solution)/shard_map/ppermute | solution.py:18
  38.1 10.9 %all-to-all-start = ((bf16[16,2,1280]{2,1,0:T(2,128)(2,1)}), bf16[16,2,1280]{2,1,0:T(2,128)(2,1)S(1)}, u32[]{:S(2)}, u32[]{:S(2)}) async-start(bf16[16,2,1280]{2,1,0:T(2,128)(2,1)} %get-tuple-element.28), calls=%async_computation | async-start | bytes 163840 | tf_op jit(solution)/shard_map/all_to_all | solution.py:395
  64.7 6.9 %collective-permute-start.14 = (bf16[32,1024]{1,0:T(8,128)(2,1)S(1)}, bf16[32,1024]{1,0:T(8,128)(2,1)S(1)}, u32[]{:S(2)}, u32[]{:S(2)}) collective-permute-start(bf16[32,1024]{1,0:T(8,128)(2,1)S(1)} %attn_out.1.refs_1_), channel_id=1, source_target_pairs={{0,12},{4,8},{8,4},{12,0},{1,13},{5,9},{9,5},{13,1},{2,14},{6,10},... | collective-permute-start | bytes 196616 | tf_op jit(solution)/shard_map/ppermute | solution.py:18
  65.2 7.5 %collective-permute-start.13 = (bf16[32,1024]{1,0:T(8,128)(2,1)S(1)}, bf16[32,1024]{1,0:T(8,128)(2,1)S(1)}, u32[]{:S(2)}, u32[]{:S(2)}) collective-permute-start(bf16[32,1024]{1,0:T(8,128)(2,1)S(1)} %attn_out.1.refs_1_), channel_id=1, source_target_pairs={{0,8},{4,12},{8,0},{12,4},{1,9},{5,13},{9,1},{13,5},{2,10},{6,14},... | collective-permute-start | bytes 196616 | tf_op jit(solution)/shard_map/ppermute | solution.py:18
  66.3 6.5 %collective-permute-start.12 = (bf16[32,1024]{1,0:T(8,128)(2,1)S(1)}, bf16[32,1024]{1,0:T(8,128)(2,1)S(1)}, u32[]{:S(2)}, u32[]{:S(2)}) collective-permute-start(bf16[32,1024]{1,0:T(8,128)(2,1)S(1)} %attn_out.1.refs_1_), channel_id=1, source_target_pairs={{0,4},{4,0},{8,12},{12,8},{1,5},{5,1},{9,13},{13,9},{2,6},{6,2},{1... | collective-permute-start | bytes 196616 | tf_op jit(solution)/shard_map/ppermute | solution.py:18
  80.1 1.5 %collective-permute-start.15 = (bf16[32,3200]{1,0:T(8,128)(2,1)S(1)}, bf16[32,3200]{1,0:T(8,128)(2,1)S(1)}, u32[]{:S(2)}, u32[]{:S(2)}) collective-permute-start(bf16[32,3200]{1,0:T(8,128)(2,1)S(1)} %get-tuple-element.31), channel_id=1, source_target_pairs={{0,1},{1,0},{2,3},{3,2},{4,5},{5,4},{6,7},{7,6},{8,9},{9,8},{10,11... | collective-permute-start | bytes 614408 | tf_op jit(solution)/shard_map/ppermute | solution.py:18
  81.8 7.1 %collective-permute-start.16 = (bf16[32,3200]{1,0:T(8,128)(2,1)S(1)}, bf16[32,3200]{1,0:T(8,128)(2,1)S(1)}, u32[]{:S(2)}, u32[]{:S(2)}) collective-permute-start(bf16[32,3200]{1,0:T(8,128)(2,1)S(1)} %pair.1.refs_0_), channel_id=1, source_target_pairs={{0,2},{1,3},{2,0},{3,1},{4,6},{5,7},{6,4},{7,5},{8,10},{9,11},{10,... | collective-permute-start | bytes 614408 | tf_op jit(solution)/shard_map/ppermute | solution.py:18
  89.2 1.4 %collective-permute-start.17 = (bf16[32,1536]{1,0:T(8,128)(2,1)S(1)}, bf16[32,1536]{1,0:T(8,128)(2,1)S(1)}, u32[]{:S(2)}, u32[]{:S(2)}) collective-permute-start(bf16[32,1536]{1,0:T(8,128)(2,1)S(1)} %hidden.1.refs_0_), channel_id=1, source_target_pairs={{0,1},{1,0},{2,3},{3,2},{4,5},{5,4},{6,7},{7,6},{8,9},{9,8},{10,11... | collective-permute-start | bytes 294920 | tf_op jit(solution)/shard_map/ppermute | solution.py:18
  95.1 4.5 %collective-permute-start.18 = (bf16[8,1024]{1,0:T(8,128)(2,1)S(1)}, bf16[8,1024]{1,0:T(8,128)(2,1)S(1)}, u32[]{:S(2)}, u32[]{:S(2)}) collective-permute-start(bf16[8,1024]{1,0:T(8,128)(2,1)S(1)} %get-tuple-element.34), channel_id=1, source_target_pairs={{0,4},{4,0},{8,12},{12,8},{1,5},{5,1},{9,13},{13,9},{2,6},{6,2},{1... | collective-permute-start | bytes 49160 | tf_op jit(solution)/shard_map/ppermute | solution.py:18
  95.7 4.6 %collective-permute-start.19 = (bf16[8,1024]{1,0:T(8,128)(2,1)S(1)}, bf16[8,1024]{1,0:T(8,128)(2,1)S(1)}, u32[]{:S(2)}, u32[]{:S(2)}) collective-permute-start(bf16[8,1024]{1,0:T(8,128)(2,1)S(1)} %get-tuple-element.35), channel_id=1, source_target_pairs={{0,8},{4,12},{8,0},{12,4},{1,9},{5,13},{9,1},{13,5},{2,10},{6,14},... | collective-permute-start | bytes 49160 | tf_op jit(solution)/shard_map/ppermute | solution.py:18
  97.2 5.5 %collective-permute-start.20 = (bf16[8,1024]{1,0:T(8,128)(2,1)S(1)}, bf16[8,1024]{1,0:T(8,128)(2,1)S(1)}, u32[]{:S(2)}, u32[]{:S(2)}) collective-permute-start(bf16[8,1024]{1,0:T(8,128)(2,1)S(1)} %get-tuple-element.36), channel_id=1, source_target_pairs={{0,12},{4,8},{8,4},{12,0},{1,13},{5,9},{9,5},{13,1},{2,14},{6,10},... | collective-permute-start | bytes 49160 | tf_op jit(solution)/shard_map/ppermute | solution.py:18
  (19 other events, 159.7 us)
